TPU v7x, 32 devices: a whole 2x2x4 slice. The times are simulated.
32 devices in a mesh: dom: 32 (over z, y, x, core).
Axes of the slice: x: 2, y: 2, z: 4, core: 2. Of those that a mesh axis runs over, the one named last changes fastest.
Arguments:
- feats: bfloat16 [196608, 128], P('dom'), may hold values from -6 to 6
- adj_vals: bfloat16 [1536, 4, 128, 128], P('dom'), may hold values from 0.0099487305 to 0.099609375
- adj_cols: int32 [1536, 4], P('dom'), may hold values from 0 to 47
- hub_feats: bfloat16 [2048, 128], P('dom'), may hold values from -6 to 6
- hub_mirrors: int32 [2048, 8], P('dom'), may hold values from 0 to 31, all different within a row; in each aligned block of 64 rows (0 to 63, 64 to 127, ...) at most 32 rows name the same one
- hub_links: int32 [2048, 8, 8], P('dom'), may hold values from 0 to 6143
- labels: int32 [196608], P('dom'), may hold values from 0 to 171
- groups: int32 [196608], P('dom'), may hold values from 0 to 63
- train_mask: int32 [196608], P('dom'), may hold values 0 or 1
- w_self: bfloat16 [128, 512], replicated, may hold values from -0.5 to 0.5
- w_neigh: bfloat16 [128, 512], replicated, may hold values from -0.5 to 0.5
- bias: float32 [512], replicated, may hold values from -3 to 3
- w_cls: bfloat16 [512, 172], replicated, may hold values from -40 to 40
- group_logw: float32 [64], replicated, may hold values from -4 to 154
Outputs:
- objective: float32 [], replicated
- grad_w_self: float32 [128, 512], replicated
- grad_w_neigh: float32 [128, 512], replicated
- grad_bias: float32 [512], replicated
- grad_w_cls: float32 [512, 172], replicated
- hub_grad: float32 [2048, 128], P('dom')
Inputs may be any that keep to these rules, and one draw needn't show every extreme that they name: `hub_mirrors`: the 8 mirrors of a hub are distinct partitions. Among the 64 hubs of one owner no partition is named by more than 32 hubs, a bound that some block reaches.
All inputs are finite; a program needn't handle non-finite values. No bound on the sum of `train_mask` on one device may be relied on, other than what follows from the above.
Results may differ from a plain program's by a relative error of at most 0.012.
The roundings to bfloat16 on the way count: a program that leaves them out, or rounds other values in their place, can miss the bound.
Values may be sent and summed in bfloat16 or wider, within the bound.
No kernel may reach another device: no remote copies, remote signals or barrier semaphores. Data moves between devices by JAX's collectives and lax.ppermute only.
A program may use at most 128 MiB of HBM per device.

v0:
```python
import jax
import jax.numpy as jnp
from jax import lax
from jax.sharding import PartitionSpec as P

drift_rate = 0.5


def spread_links(source_rows, targets, dump_row):
    totals = jnp.zeros((dump_row + 1, source_rows.shape[1]), jnp.float32)
    counted = jnp.zeros((dump_row + 1,), jnp.float32)
    unit_rows = jnp.ones((targets.shape[0],), jnp.float32)
    for link_index in range(targets.shape[1]):
        totals = totals + jax.ops.segment_sum(
            source_rows, targets[:, link_index], num_segments=dump_row + 1
        )
        counted = counted + jax.ops.segment_sum(
            unit_rows, targets[:, link_index], num_segments=dump_row + 1
        )
    return (totals[:dump_row], counted[:dump_row])


def gather_links(values, targets):
    padded = jnp.concatenate([values, jnp.zeros((1, values.shape[1]), jnp.float32)], axis=0)
    totals = jnp.zeros((targets.shape[0], values.shape[1]), jnp.float32)
    for link_index in range(targets.shape[1]):
        totals = totals + padded[targets[:, link_index]]
    return totals


def local_sums(feats_part, vals_part, cols_part):
    row_blocks = cols_part.shape[0]
    tile_side = vals_part.shape[2]
    blocks = feats_part.reshape(row_blocks, tile_side, -1)
    picked = blocks[cols_part]
    summed = jnp.einsum("rkij,rkjf->rif", vals_part, picked, preferred_element_type=jnp.float32)
    weight_mass = jnp.sum(vals_part.astype(jnp.float32), axis=(1, 3))
    return (summed.reshape(row_blocks * tile_side, -1), weight_mass.reshape(-1))


def on_device(
    feats,
    adj_vals,
    adj_cols,
    hub_feats,
    hub_mirrors,
    hub_links,
    labels,
    groups,
    train_mask,
    w_self,
    w_neigh,
    bias,
    w_cls,
    group_logw,
):
    vert_rows = feats.shape[0]
    width = feats.shape[1]
    n_dom = lax.axis_size("dom")
    hub_dev = hub_feats.shape[0]
    mirror_count = hub_mirrors.shape[1]
    link_count = hub_links.shape[2]
    group_total = group_logw.shape[0]
    class_total = w_cls.shape[1]
    group_ids = jnp.arange(group_total)
    class_ids = jnp.arange(class_total)
    mask_float = train_mask.astype(jnp.float32)
    group_hot = (groups[:, None] == group_ids[None, :]).astype(jnp.float32)
    count_local = jnp.sum(mask_float[:, None] * group_hot, axis=0)
    capacity = min(hub_dev, max(2, 2 * hub_dev * mirror_count // n_dom))
    pair_total = hub_dev * mirror_count
    pair_dest = hub_mirrors.reshape(pair_total)
    dest_hot = (pair_dest[:, None] == jnp.arange(n_dom)[None, :]).astype(jnp.int32)
    pair_rank = jnp.sum((jnp.cumsum(dest_hot, axis=0) - 1) * dest_hot, axis=1)
    slot_index = pair_dest * capacity + pair_rank
    repeated = jnp.broadcast_to(hub_feats[:, None, :], (hub_dev, mirror_count, width)).reshape(
        pair_total, width
    )
    send_feats = jnp.zeros((n_dom * capacity, width), jnp.bfloat16).at[slot_index].set(repeated)
    send_links = (
        jnp.full((n_dom * capacity, link_count), -1, jnp.int32)
        .at[slot_index]
        .set(hub_links.reshape(pair_total, link_count))
    )
    recv_feats, recv_links = (
        lax.all_to_all(
            send_feats.reshape(n_dom, capacity, width),
            "dom",
            split_axis=0,
            concat_axis=0,
            tiled=True,
        ),
        lax.all_to_all(
            send_links.reshape(n_dom, capacity, link_count),
            "dom",
            split_axis=0,
            concat_axis=0,
            tiled=True,
        ),
    )
    recv_links = recv_links.reshape(n_dom * capacity, link_count)
    targets = jnp.where(recv_links >= 0, recv_links, vert_rows).astype(jnp.int32)
    source_rows = recv_feats.reshape(n_dom * capacity, width).astype(jnp.float32)
    local, mass = local_sums(feats, adj_vals, adj_cols)
    hub_sum, hub_hits = spread_links(source_rows, targets, vert_rows)
    denom = 1.0 + mass + hub_hits
    agg = ((feats.astype(jnp.float32) + local + hub_sum) / denom[:, None]).astype(jnp.bfloat16)
    pre = (
        jnp.dot(feats, w_self, preferred_element_type=jnp.float32)
        + jnp.dot(agg, w_neigh, preferred_element_type=jnp.float32)
        + bias
    )
    hidden = jnp.maximum(pre, 0.0).astype(jnp.bfloat16)
    logits = jnp.dot(hidden, w_cls, preferred_element_type=jnp.float32)
    label_hot = (labels[:, None] == class_ids[None, :]).astype(jnp.float32)
    loss = (jax.nn.logsumexp(logits, axis=1) - jnp.sum(logits * label_hot, axis=1)) * mask_float
    loss_local = jnp.sum(loss[:, None] * group_hot, axis=0)
    gsum, count_total = lax.psum((loss_local, count_local), "dom")
    weights = group_total * jax.nn.softmax(group_logw + drift_rate * gsum / (count_total + 1.0))
    objective = jnp.sum(weights * gsum)
    vertex_weight = mask_float * jnp.sum(group_hot * weights[None, :], axis=1)
    probs = jax.nn.softmax(logits, axis=1)
    dlogits = (vertex_weight[:, None] * (probs - label_hot)).astype(jnp.bfloat16)
    gwc = jnp.dot(hidden.T, dlogits, preferred_element_type=jnp.float32)
    dhidden = jnp.dot(dlogits, w_cls.T, preferred_element_type=jnp.float32)
    dpre_full = jnp.where(pre > 0.0, dhidden, 0.0)
    gbias = jnp.sum(dpre_full, axis=0)
    dpre = dpre_full.astype(jnp.bfloat16)
    gws = jnp.dot(feats.T, dpre, preferred_element_type=jnp.float32)
    gwn = jnp.dot(agg.T, dpre, preferred_element_type=jnp.float32)
    dagg = jnp.dot(dpre, w_neigh.T, preferred_element_type=jnp.float32)
    dsum = dagg / denom[:, None]
    slot_grads = gather_links(dsum, targets)
    returned = lax.all_to_all(
        slot_grads.reshape(n_dom, capacity, width), "dom", split_axis=0, concat_axis=0, tiled=True
    )
    returned = returned.reshape(n_dom * capacity, width)
    hub_grad = jnp.sum(returned[slot_index].reshape(hub_dev, mirror_count, width), axis=1)
    grad_w_self, grad_w_neigh, grad_bias, grad_w_cls = lax.psum((gws, gwn, gbias, gwc), "dom")
    return (objective, grad_w_self, grad_w_neigh, grad_bias, grad_w_cls, hub_grad)


def solution(mesh):
    in_specs = (
        P("dom", None),
        P("dom", None, None, None),
        P("dom", None),
        P("dom", None),
        P("dom", None),
        P("dom", None, None),
        P("dom"),
        P("dom"),
        P("dom"),
        P(),
        P(),
        P(),
        P(),
        P(),
    )
    out_specs = (P(), P(), P(), P(), P(), P("dom", None))
    return jax.shard_map(
        on_device, mesh=mesh, in_specs=in_specs, out_specs=out_specs, check_vma=False
    )
```

profile of v0, /device:TPU:0, one launch (start us, length us, event | category | flops | bytes accessed | tf_op | source)
XLA Modules:
  0.0 462.5 jit_solution(3339118693778942036)
XLA Ops:
  9.1 1.2 reduce-window.6
  10.5 0.9 copy.67
  11.5 1.9 scatter_custom_fusion
  14.3 7.3 %all-to-all-start = ((s32[32,1,256]{2,1,0:T(1,128)}), s32[32,1,256]{2,1,0:T(1,128)S(1)}, u32[]{:S(2)}, u32[]{:S(2)}) async-start(s32[32,1,256]{2,1,0:T(1,128)} %reshape.299), calls=%async_computation | async-start | bytes 65536 | tf_op jit(solution)/shard_map/all_to_all | solution.py:93
  21.6 3.8 convert_reduce_fusion
  25.5 6.4 %fusion.36 = f32[6144,512]{1,0:T(8,128)} fusion(bf16[6144,128]{1,0:T(8,128)(2,1)S(1)} %copy-done.2, bf16[128,512]{1,0:T(8,128)(2,1)S(1)} %copy-done.11), kind=kOutput, calls=%fused_computation.120 | convolution fusion | flops 805306368 | bytes 14286848 | tf_op jit(solution)/shard_map/dot_general | solution.py:109
  32.1 2.4 scatter_custom_fusion.1
  34.6 5.8 %all-to-all-start.1 = ((bf16[32,32,128]{2,1,0:T(8,128)(2,1)}), bf16[32,32,128]{2,1,0:T(8,128)(2,1)S(1)}, u32[]{:S(2)}, u32[]{:S(2)}) async-start(bf16[32,32,128]{2,1,0:T(8,128)(2,1)} %bitcast.13), calls=%async_computation.1 | async-start | bytes 524288 | tf_op jit(solution)/shard_map/all_to_all | solution.py:86
  42.1 6.7 %scatter_custom_fusion.6 = f32[6145]{0:T(1024)S(1)} fusion(s32[1024]{0:T(1024)S(1)} %bitcast.106, f32[1024]{0:T(1024)S(1)} %broadcast_in_dim.22, f32[]{:T(128)} %constant.15.clone.1), kind=kCustom, calls=%fused_computation.88 | custom fusion | flops 1024 | bytes 24584 | tf_op jit(solution)/shard_map/scatter-add | solution.py:17
  48.7 37.0 %scatter_custom_fusion.5 = f32[6145]{0:T(1024)S(1)} fusion(s32[6144]{0:T(1024)S(1)} %bitcast.108, f32[6144]{0:T(1024)S(1)} %pad.34, f32[]{:T(128)} %constant.15.clone.1), kind=kCustom, calls=%fused_computation.90 | custom fusion | flops 6144 | bytes 24584 | tf_op jit(solution)/shard_map/add | solution.py:17
  85.8 7.1 %scatter_fusion = f32[6145]{0:T(1024)S(1)} fusion(f32[6145]{0:T(1024)S(1)} %add.244, s32[1024]{0:T(1024)S(1)} %bitcast.92, f32[1024]{0:T(1024)S(1)} %broadcast_in_dim.22), kind=kCustom, calls=%fused_computation.17 | custom fusion | flops 1024 | bytes 16384 | tf_op jit(solution)/shard_map/scatter-add | solution.py:17
  92.9 8.0 %gather_fusion = bf16[192,128,128]{2,1,0:T(8,128)(2,1)} fusion(bf16[48,128,128]{2,1,0:T(8,128)(2,1)S(1)} %bitcast.77, s32[1024]{0:T(1024)S(1)} %get-tuple-element.71), kind=kCustom, calls=%fused_computation | custom fusion | bytes 12583680 | tf_op jit(solution)/shard_map/gather | solution.py:35
  100.9 8.1 %fusion.37 = f32[48,128,128,1]{1,2,3,0:T(8,128)} fusion(bf16[48,4,128,128]{3,2,1,0:T(8,128)(2,1)} %param.15, bf16[48,4,128,128]{3,2,1,0:T(8,128)(2,1)} %bitcast.78), kind=kOutput, calls=%fused_computation.121 | convolution fusion | flops 805306368 | bytes 15728640 | tf_op jit(solution)/shard_map/rkij,rkjf->rif/dot_general | solution.py:36
  109.0 8.2 %scatter_custom_fusion.3 = f32[6145,128]{1,0:T(8,128)} fusion(s32[1024]{0:T(1024)S(1)} %bitcast.107, f32[]{:T(128)} %constant.15.clone.1, bf16[1024,128]{1,0:T(8,128)(2,1)S(1)} %bitcast.81), kind=kCustom, calls=%fused_computation.35 | custom fusion | flops 262144 | bytes 3408388 | tf_op jit(solution)/shard_map/scatter-add | solution.py:14
  118.1 0.8 convert_dynamic-update-slice_fusion.3
  119.7 0.8 convert_dynamic-update-slice_fusion.1
  121.4 0.9 convert_dynamic-update-slice_fusion.5
  122.3 37.4 %scatter_custom_fusion.2 = f32[6145,128]{1,0:T(8,128)} fusion(s32[6144]{0:T(1024)S(1)} %bitcast.109, f32[6144,128]{1,0:T(8,128)} %convert_dynamic-update-slice_fusion.5, f32[]{:T(128)} %constant.15.clone.1), kind=kCustom, calls=%fused_computation.37 | custom fusion | flops 786432 | bytes 3146752 | tf_op jit(solution)/shard_map/add | solution.py:14
  159.6 4.8 %add.238 = f32[6145,128]{1,0:T(8,128)} add(f32[6145,128]{1,0:T(8,128)} %scatter_custom_fusion.2, f32[6145,128]{1,0:T(8,128)} %scatter_custom_fusion.3) | non-fusion elementwise | flops 786560 | bytes 9438720 | tf_op jit(solution)/shard_map/add | solution.py:14
  164.5 9.8 %scatter_custom_fusion.4 = f32[6145,128]{1,0:T(8,128)} fusion(f32[6145,128]{1,0:T(8,128)} %add.238, s32[1024]{0:T(1024)S(1)} %bitcast.93, bf16[1024,128]{1,0:T(8,128)(2,1)S(1)} %bitcast.88), kind=kCustom, calls=%fused_computation.48 | custom fusion | flops 262144 | bytes 3408384 | tf_op jit(solution)/shard_map/scatter-add | solution.py:14
  174.3 3.4 fusion.2
  177.7 6.9 %add_add_fusion = f32[6144,512]{1,0:T(8,128)S(1)} fusion(f32[6144,512]{1,0:T(8,128)} %fusion.36, bf16[6144,128]{1,0:T(8,128)(2,1)S(1)} %fusion.2, bf16[128,512]{1,0:T(8,128)(2,1)S(1)} %copy-done.12, f32[512]{0:T(512)S(1)} %copy-done.16), kind=kOutput, calls=%fused_computation.19 | convolution fusion | flops 811597824 | bytes 26871808 | tf_op jit(solution)/shard_map/dot_general | solution.py:110
  184.7 2.3 fusion.34
  187.0 2.2 copy-done.1
  189.3 2.0 copy-done.4
  191.2 1.8 fusion
  193.6 53.9 %all-reduce.6 = (f32[64]{0:T(128)S(1)}, f32[64]{0:T(128)S(1)}) all-reduce(f32[64]{0:T(128)S(1)} %get-tuple-element.46, f32[64]{0:T(128)S(1)} %get-tuple-element.45), channel_id=1, replica_groups=mesh['dom'=32] {'dom'}, use_global_device_ids=true, to_apply=%region_18.19 | all-reduce | flops 128 | bytes 1024 | tf_op jit(solution)/shard_map/psum | solution.py:118
  248.1 1.2 fusion.32
  249.4 1.9 multiply_reduce_fusion
  251.6 8.6 %fusion.3 = f32[512,172]{0,1:T(8,128)} fusion(f32[6144,512]{1,0:T(8,128)} %copy-done.1, f32[6144,172]{0,1:T(8,128)} %copy-done.4, f32[6144]{0:T(1024)S(1)} %get-tuple-element.42, f32[6144]{0:T(1024)S(1)} %get-tuple-element.67, f32[6144]{0:T(1024)S(1)} %convert_multiply_fusion, s32[6144]{0:T(1024)S(1)} %copy-done.14), kind=kOutput, calls=%fused_computation.33 | convolution fusion | flops 1095819264 | bytes 17260544 | tf_op jit(solution)/shard_map/dot_general | solution.py:124
  260.2 6.4 %fusion.35 = (f32[512]{0:T(512)S(1)}, bf16[6144,512]{1,0:T(8,128)(2,1)S(1)}) fusion(bf16[512,172]{0,1:T(8,128)(2,1)S(1)} %copy-done, f32[6144,172]{0,1:T(8,128)S(1)} %bitcast.80, f32[6144]{0:T(1024)S(1)} %get-tuple-element.42, f32[6144]{0:T(1024)S(1)} %get-tuple-element.67, f32[6144]{0:T(1024)S(1)} %convert_multiply_fusion, s32[6144]{0:T(1024)S(1)} %copy-done.14, ...), kind=kOutput, calls=%fused_computation.119 | convolution fusion | flops 1102110208 | bytes 23377920 | tf_op jit(solution)/shard_map/dot_general | solution.py:125
  266.6 1.8 convolution_divide_fusion
  269.5 4.0 gather_fusion.8
  273.5 4.0 gather_fusion.7
  277.5 4.0 gather_fusion.6
  281.4 4.0 gather_fusion.5
  285.4 4.0 gather_fusion.4
  289.4 4.0 gather_fusion.3
  293.4 4.0 gather_fusion.2
  297.4 4.0 gather_fusion.1
  301.4 3.2 add_add_fusion.1
  304.6 3.7 all-to-all-start.2
  308.4 4.6 fusion.27
  313.1 5.3 %convolution_bitcast_fusion = f32[128,512]{0,1:T(8,128)} fusion(bf16[6144,128]{1,0:T(8,128)(2,1)S(1)} %copy-done.3, bf16[6144,512]{1,0:T(8,128)(2,1)} %copy-done.7), kind=kOutput, calls=%fused_computation.52 | convolution fusion | flops 805306368 | bytes 8126464 | tf_op jit(solution)/shard_map/dot_general | solution.py:129
  318.4 40.7 %psum.46 = f32[512]{0:T(512)} all-reduce(f32[512]{0:T(512)S(1)} %get-tuple-element.69), channel_id=1, replica_groups=mesh['dom'=32] {'dom'}, use_global_device_ids=true, to_apply=%region_27.28 | all-reduce | flops 512 | bytes 4096 | tf_op jit(solution)/shard_map/psum | solution.py:139
  359.1 90.3 %all-reduce.10.cloned.1.call-done = (f32[128,512]{0,1:T(8,128)}, f32[128,512]{1,0:T(8,128)}, f32[512,172]{0,1:T(8,128)}) async-done(((f32[128,512]{0,1:T(8,128)}, f32[128,512]{1,0:T(8,128)}, f32[512,172]{0,1:T(8,128)}), (f32[128,512]{0,1:T(8,128)}, f32[128,512]{1,0:T(8,128)}, f32[512,172]{0,1:T(8,128)})) %all-reduce.10.cloned.1.call-update) | async-done | bytes 876560 | tf_op jit(solution)/shard_map/psum | solution.py:139
  449.4 1.8 copy.65
  451.3 2.1 gather_fusion.9
  (99 shorter events, 12.2 us)
Async XLA Ops:
  7.2 177.5 %copy-start = (bf16[512,172]{0,1:T(8,128)(2,1)S(1)}, bf16[512,172]{0,1:T(8,128)(2,1)}, u32[]{:S(2)}) copy-start(bf16[512,172]{0,1:T(8,128)(2,1)} %param.26) | copy-start | bytes 528388
  14.3 20.3 %all-to-all-start = ((s32[32,1,256]{2,1,0:T(1,128)}), s32[32,1,256]{2,1,0:T(1,128)S(1)}, u32[]{:S(2)}, u32[]{:S(2)}) async-start(s32[32,1,256]{2,1,0:T(1,128)} %reshape.299), calls=%async_computation | async-start | bytes 65536 | tf_op jit(solution)/shard_map/all_to_all | solution.py:93
  21.6 3.9 copy-start.2
  21.6 3.9 copy-start.11
  25.5 6.4 %copy-start.17 = (s32[48,4]{0,1:T(4,128)S(1)}, s32[48,4]{0,1:T(4,128)}, u32[]{:S(2)}) copy-start(s32[48,4]{0,1:T(4,128)} %param.16) | copy-start | bytes 2308
  25.5 6.6 %copy-start.10 = (s32[6144]{0:T(1024)S(1)}, s32[6144]{0:T(1024)}, u32[]{:S(2)}) copy-start(s32[6144]{0:T(1024)} %param.22) | copy-start | bytes 73732
  25.5 6.6 %copy-start.15 = (bf16[64,128]{1,0:T(8,128)(2,1)S(1)}, bf16[64,128]{1,0:T(8,128)(2,1)}, u32[]{:S(2)}) copy-start(bf16[64,128]{1,0:T(8,128)(2,1)} %param.17) | copy-start | bytes 49156
  34.6 74.4 %all-to-all-start.1 = ((bf16[32,32,128]{2,1,0:T(8,128)(2,1)}), bf16[32,32,128]{2,1,0:T(8,128)(2,1)S(1)}, u32[]{:S(2)}, u32[]{:S(2)}) async-start(bf16[32,32,128]{2,1,0:T(8,128)(2,1)} %bitcast.13), calls=%async_computation.1 | async-start | bytes 524288 | tf_op jit(solution)/shard_map/all_to_all | solution.py:86
  174.3 3.4 copy-start.12
  174.3 3.4 copy-start.16
  177.7 7.0 %copy-start.5 = (bf16[6144,128]{1,0:T(8,128)(2,1)}, bf16[6144,128]{1,0:T(8,128)(2,1)S(1)}, u32[]{:S(2)}) copy-start(bf16[6144,128]{1,0:T(8,128)(2,1)S(1)} %fusion.2) | copy-start | bytes 4718596
  184.7 4.6 copy-start.1
  184.7 6.5 %copy-start.14 = (s32[6144]{0:T(1024)S(1)}, s32[6144]{0:T(1024)}, u32[]{:S(2)}) copy-start(s32[6144]{0:T(1024)} %param.20) | copy-start | bytes 73732
  189.2 2.0 copy-start.4
  189.3 3.8 copy-start.13
  189.3 58.3 %copy-start.18 = (f32[64]{0:T(128)S(1)}, f32[64]{0:T(128)}, u32[]{:S(2)}) copy-start(f32[64]{0:T(128)} %param.27) | copy-start | bytes 772
  193.1 67.1 %slice-start = ((s8[4325376]{0:T(1024)(128)(4,1)}), s8[131072]{0:T(1024)(128)(4,1)S(1)}, s32[]{:S(2)}) async-start(s8[4325376]{0:T(1024)(128)(4,1)} %bitcast.79), calls=%async_computation.4 | async-start | bytes 262144
  251.6 8.6 %slice-start.1 = ((s8[4325376]{0:T(1024)(128)(4,1)}), s8[4194304]{0:T(1024)(128)(4,1)S(1)}, s32[]{:S(2)}) async-start(s8[4325376]{0:T(1024)(128)(4,1)} %bitcast.79), calls=%async_computation.5 | async-start | bytes 8388608
  266.6 2.6 copy-start.7
  301.4 7.1 %copy-start.6 = (bf16[6144,128]{1,0:T(8,128)(2,1)S(1)}, bf16[6144,128]{1,0:T(8,128)(2,1)}, u32[]{:S(2)}) copy-start(bf16[6144,128]{1,0:T(8,128)(2,1)} %copy-done.5) | copy-start | bytes 4718596
  304.6 146.7 %all-to-all-start.2 = ((f32[32,32,128]{2,1,0:T(8,128)}), f32[32,32,128]{2,1,0:T(8,128)}, u32[]{:S(2)}, u32[]{:S(2)}) async-start(f32[32,32,128]{2,1,0:T(8,128)} %bitcast.28), calls=%async_computation.2 | async-start | bytes 1048576 | tf_op jit(solution)/shard_map/all_to_all | solution.py:134
  308.4 4.7 %copy-start.3 = (bf16[6144,128]{1,0:T(8,128)(2,1)S(1)}, bf16[6144,128]{1,0:T(8,128)(2,1)}, u32[]{:S(2)}) copy-start(bf16[6144,128]{1,0:T(8,128)(2,1)} %param.14) | copy-start | bytes 4718596
  308.4 141.0 %all-reduce.10.cloned.1.call-start = ((), (), s32[]{:S(2)}) async-start(), calls=%async_computation.3 | async-start | bytes 1769472 | tf_op jit(solution)/shard_map/psum | solution.py:139
  449.4 4.6 copy-start.9
  449.4 5.3 %copy-start.8 = (f32[512,172]{0,1:T(8,128)S(1)}, f32[512,172]{0,1:T(8,128)}, u32[]{:S(2)}) copy-start(f32[512,172]{0,1:T(8,128)} %get-tuple-element.85) | copy-start | bytes 1056772
Sparse Core Ops, SparseCore 0:
  318.5 130.8 all-reduce.9
where the time goes:
time: 471 us; the launch traced here: 463 us
  other arithmetic  136 us (29%)
  blocking collectives  94.6 us (20%)
  waiting for transfers between devices  90.3 us (19%)
  local copies, waits for them, and re-layouts  59.1 us (13%)
  matrix products  50.4 us (11%)
  starting transfers between devices  16.9 us (4%)
  between operations  14.7 us (3%)
    psum x1, waiting for transfers between devices, on_device(): lax.psum((gws, gwn, gbias, gwc), 'dom')  90.3 us
    psum x1, blocking collectives, on_device(): gsum, count_total = lax.psum((loss_local, count_local), 'dom')  53.9 us
    add x2, other arithmetic, spread_links(): totals + jax.ops.segment_sum(source_rows, targets[:, link_index], num_seg...  42.2 us
    psum x1, blocking collectives, on_device(): lax.psum((gws, gwn, gbias, gwc), 'dom')  40.7 us
    add x2, other arithmetic, spread_links(): counted + jax.ops.segment_sum(unit_rows, targets[:, link_index], num_segm...  37 us
    gather x8, local copies, waits for them, and re-layouts, gather_links(): totals = totals + padded[targets[:, link_index]]  31.9 us
    scatter-add x2, other arithmetic, spread_links(): jax.ops.segment_sum(source_rows, targets[:, link_index], num_segments=dum...  18.1 us
    scatter-add x2, other arithmetic, spread_links(): jax.ops.segment_sum(unit_rows, targets[:, link_index], num_segments=dump_...  13.8 us
  transfers between devices with their start and end apart: 4, of which 1 were waited for; matrix products, arithmetic and copies ran while one was open for 20% of the time, Pallas kernels for 0%

commit v1 on v0

v1 whole, which is shorter than its diff:
```python
import functools

import jax
import jax.numpy as jnp
from jax import lax
from jax.experimental import pallas as pl
from jax.experimental.pallas import tpu as pltpu
from jax.sharding import PartitionSpec as P

drift_rate = 0.5
LANES = 128
F32 = jnp.float32
BF16 = jnp.bfloat16
I32 = jnp.int32


def dot_nn(a, b):
    return lax.dot_general(a, b, (((1,), (0,)), ((), ())), preferred_element_type=F32)


def dot_nt(a, b):
    return lax.dot_general(a, b, (((1,), (1,)), ((), ())), preferred_element_type=F32)


def dot_tn(a, b):
    return lax.dot_general(a, b, (((0,), (0,)), ((), ())), preferred_element_type=F32)


def iota(shape, dim):
    return lax.broadcasted_iota(I32, shape, dim)


def params(n_grid=0, mib=56):
    kw = {} if n_grid == 0 else {"dimension_semantics": ("arbitrary",) * n_grid}
    return pltpu.CompilerParams(vmem_limit_bytes=mib << 20, **kw)


def pack_kernel(n, cap, me_ref, hub_ref, mir_ref, link_ref, out_ref, place_ref):
    hubs, width = hub_ref.shape
    mirrors, links = link_ref.shape[0], link_ref.shape[1]
    dest = iota((n, hubs), 0)
    present = jnp.zeros((n, hubs), F32)
    for j in range(mirrors):
        present = present + jnp.where(mir_ref[j : j + 1, :] == dest, 1.0, 0.0)
    before = jnp.where(iota((hubs, hubs), 0) < iota((hubs, hubs), 1), 1.0, 0.0)
    rank = dot_nn(present.astype(BF16), before.astype(BF16))
    rank = jnp.where(present > 0.0, rank, 9999.0).astype(I32)
    place = jnp.where(rank[:, None, :] == iota((n, cap, hubs), 1), 1.0, 0.0)
    place = place.reshape(n * cap, hubs).astype(BF16)
    place_ref[...] = place
    rows = dot_nn(place, hub_ref[...])
    out_ref[:, 0:cap, :] = rows.reshape(n, cap, width).astype(BF16)
    dest3 = iota((n, links, hubs), 0)
    ends = jnp.zeros((n, links, hubs), I32)
    for j in range(mirrors):
        ends = ends + jnp.where(mir_ref[j : j + 1, :][None] == dest3, link_ref[j][None], 0)
    high = ((ends >> 7) + 1).astype(F32)
    low = (ends & 127).astype(F32)
    both = jnp.concatenate([high, low], axis=1).astype(BF16)
    offset = (me_ref[0] * cap) % LANES
    lane_of = rank[:, None, :] + offset == iota((n, LANES, hubs), 1)
    lane_of = jnp.where(lane_of, 1.0, 0.0).astype(BF16)
    packed = lax.dot_general(
        both, lane_of, (((2,), (2,)), ((0,), (0,))), preferred_element_type=F32
    )
    out_ref[:, cap : cap + 2 * links, :] = packed.astype(BF16)


def local_kernel(tiles, cols_ref, feats_ref, vals_ref, s_ref, ft_ref, mass_ref, turned):
    step = pl.program_id(0)
    width = feats_ref.shape[1]
    blocks = turned.shape[0]

    @pl.when(step == 0)
    def _():
        def turn(b, carry):
            rows = feats_ref[pl.ds(pl.multiple_of(b * LANES, LANES), LANES), :]
            turned[b, 0:width, :] = rows.astype(F32).T.astype(BF16)
            turned[b, width:, :] = jnp.ones((16, LANES), BF16)
            return carry

        lax.fori_loop(0, blocks, turn, 0, unroll=4)

    per_step = vals_ref.shape[0]
    for r in range(per_step):
        block = step * per_step + r
        left = jnp.concatenate([turned[cols_ref[block, k]] for k in range(tiles)], axis=1)
        right = jnp.concatenate([vals_ref[r, k] for k in range(tiles)], axis=1)
        both = dot_nt(left, right)
        own = turned[block, 0:width, :]
        span = slice(r * LANES, (r + 1) * LANES)
        s_ref[:, span] = own.astype(F32) + both[0:width]
        ft_ref[:, span] = own
        mass_ref[:, span] = both[width : width + 8]


def lane_row(ref, step, parts):
    return jnp.concatenate([ref[pl.ds(step * parts + k, 1), :] for k in range(parts)], axis=1)


def fold_lanes(x):
    total = x[:, 0:LANES]
    for k in range(1, x.shape[1] // LANES):
        total = total + x[:, k * LANES : (k + 1) * LANES]
    return total


def forward_kernel(
    n, cap, links, classes, span,
    recv_ref, s_ref, ft_ref, mass_ref, label_ref, group_ref, mask_ref, w_ref, bias_ref, wc_ref,
    fa_ref, hid_ref, pmo_ref, m_ref, inv_ref, sums_ref,
    src, word_of, value_of, loss_acc, count_acc,
):
    step = pl.program_id(0)
    slots = n * cap
    width = s_ref.shape[0]
    groups = loss_acc.shape[0]
    parts = span // LANES

    @pl.when(step == 0)
    def _():
        loss_acc[...] = jnp.zeros_like(loss_acc)
        count_acc[...] = jnp.zeros_like(count_acc)
        per = LANES // cap
        for b in range(slots // LANES):
            rows = recv_ref[b * per : (b + 1) * per, 0:cap, :].astype(F32).reshape(LANES, width)
            src[0:width, b * LANES : (b + 1) * LANES] = rows.T.astype(BF16)
            ends = recv_ref[b * per, cap : cap + 2 * links, :].astype(F32)
            for k in range(1, per):
                ends = ends + recv_ref[b * per + k, cap : cap + 2 * links, :].astype(F32)
            target = ((ends[0:links] - 1.0) * 128.0 + ends[links:]).astype(I32)
            word_of[:, b * LANES : (b + 1) * LANES] = target >> 3
            value_of[:, b * LANES : (b + 1) * LANES] = jnp.left_shift(1, (target & 7) * 4)
        src[width:, :] = jnp.ones((16, slots), BF16)

    chunk = 256
    for b in range(parts):
        first = (step * span + b * LANES) // 8
        for c in range(slots // chunk):
            at = slice(c * chunk, (c + 1) * chunk)
            rows16 = iota((16, chunk), 0) + first
            words = jnp.zeros((16, chunk), I32)
            for k in range(links):
                words = words + jnp.where(
                    word_of[k : k + 1, at] == rows16, value_of[k : k + 1, at], 0
                )
            wide = jnp.broadcast_to(words[:, None, :], (16, 8, chunk))
            count = (wide >> (4 * iota((16, 8, chunk), 1))) & 15
            m_ref[b * LANES : (b + 1) * LANES, at] = (
                count.reshape(LANES, chunk).astype(F32).astype(BF16)
            )
    hub = dot_nt(src[...], m_ref[...])
    denom = 1.0 + mass_ref[0:1, :] + hub[width : width + 1, :]
    inverse = 1.0 / denom
    inv_ref[...] = jnp.broadcast_to(inverse, inv_ref.shape)
    agg = ((s_ref[...] + hub[0:width]) * inverse).astype(BF16)
    fa_ref[0:width, :] = ft_ref[...]
    fa_ref[width:, :] = agg
    pre = dot_nn(w_ref[...], fa_ref[...]) + bias_ref[:, 0:1]
    hidden = jnp.maximum(pre, 0.0).astype(BF16)
    hid_ref[...] = hidden
    logits = dot_nn(wc_ref[...], hidden)
    class_row = iota(logits.shape, 0)
    logits = jnp.where(class_row < classes, logits, -jnp.inf)
    top = jnp.max(logits, axis=0, keepdims=True)
    shifted = jnp.exp(logits - top)
    total = jnp.sum(shifted, axis=0, keepdims=True)
    mask = lane_row(mask_ref, step, parts).astype(F32)
    hot = class_row == lane_row(label_ref, step, parts)
    picked = jnp.sum(jnp.where(hot, logits, 0.0), axis=0, keepdims=True)
    loss = (top + jnp.log(total) - picked) * mask
    pmo_ref[...] = mask * (shifted * (1.0 / total) - jnp.where(hot, 1.0, 0.0))
    in_group = iota((groups, span), 0) == lane_row(group_ref, step, parts)
    loss_acc[...] += fold_lanes(jnp.where(in_group, loss, 0.0))
    count_acc[...] += fold_lanes(jnp.where(in_group, mask, 0.0))

    @pl.when(step == pl.num_programs(0) - 1)
    def _():
        sub, lane = iota((groups, LANES), 0), iota((groups, LANES), 1)
        loss_col = jnp.sum(loss_acc[...], axis=1, keepdims=True)
        count_col = jnp.sum(count_acc[...], axis=1, keepdims=True)
        both = jnp.where(lane == sub, loss_col, 0.0) + jnp.where(
            lane == sub + groups, count_col, 0.0
        )
        row = jnp.sum(both, axis=0, keepdims=True)
        sums_ref[...] = jnp.broadcast_to(row[None], sums_ref.shape)


def backward_kernel(
    n, cap, share, span,
    sums_ref, logw_ref, pmo_ref, hid_ref, fa_ref, m_ref, inv_ref, group_ref, wc_ref, wn_ref,
    msg_ref, obj_ref,
    q_col, gw, gwc, gb, slot, flat,
):
    step = pl.program_id(0)
    groups = logw_ref.shape[1]
    slots = n * cap
    parts = span // LANES
    hidden_rows = gb.shape[0]
    both_rows = fa_ref.shape[0]
    class_rows = pmo_ref.shape[0]

    @pl.when(step == 0)
    def _():
        row = jnp.sum(sums_ref[...], axis=0)
        sub, lane = iota((groups, LANES), 0), iota((groups, LANES), 1)
        gsum = jnp.sum(jnp.where(lane == sub, row, 0.0), axis=1, keepdims=True)
        gcount = jnp.sum(jnp.where(lane == sub + groups, row, 0.0), axis=1, keepdims=True)
        sub, lane = iota((groups, groups), 0), iota((groups, groups), 1)
        logw = jnp.sum(jnp.where(lane == sub, logw_ref[...], 0.0), axis=1, keepdims=True)
        score = logw + drift_rate * gsum / (gcount + 1.0)
        e = jnp.exp(score - jnp.max(score, axis=0, keepdims=True))
        q = groups * (e / jnp.sum(e, axis=0, keepdims=True))
        obj_ref[0, 0] = jnp.sum(q * gsum)
        q_col[...] = jnp.broadcast_to(q, q_col.shape)
        gw[...] = jnp.zeros_like(gw)
        gwc[...] = jnp.zeros_like(gwc)
        gb[...] = jnp.zeros_like(gb)
        slot[...] = jnp.zeros_like(slot)

    in_group = iota((groups, span), 0) == lane_row(group_ref, step, parts)
    weight = jnp.sum(jnp.where(in_group, q_col[:, 0:1], 0.0), axis=0, keepdims=True)
    dlogits = (pmo_ref[...] * weight).astype(BF16)
    hidden = hid_ref[...]
    gwc[...] += dot_nt(dlogits, hidden)
    dhidden = dot_nn(wc_ref[...], dlogits)
    dfull = jnp.where(hidden.astype(F32) > 0.0, dhidden, 0.0)
    gb[...] += fold_lanes(dfull)
    dpre = dfull.astype(BF16)
    gw[...] += dot_nt(fa_ref[...], dpre)
    dagg = dot_nn(wn_ref[...], dpre)
    dsum = (dagg * inv_ref[0:1, :]).astype(BF16)
    slot[...] += dot_nn(dsum, m_ref[...])

    @pl.when(step == pl.num_programs(0) - 1)
    def _():
        per = LANES // cap
        for b in range(slots // LANES):
            rows = slot[:, b * LANES : (b + 1) * LANES].T
            msg_ref[b * per : (b + 1) * per, 0:cap, :] = rows.reshape(per, cap, LANES).astype(BF16)
        row = 0
        for b in range(hidden_rows // LANES):
            flat[row : row + both_rows, :] = gw[:, b * LANES : (b + 1) * LANES]
            row += both_rows
        for b in range(hidden_rows // LANES):
            flat[row : row + class_rows, :] = gwc[:, b * LANES : (b + 1) * LANES]
            row += class_rows
        flat[row:, :] = jnp.zeros((flat.shape[0] - row, LANES), F32)
        sub, lane = iota((LANES, LANES), 0), iota((LANES, LANES), 1)
        for b in range(hidden_rows // LANES):
            col = jnp.sum(gb[b * LANES : (b + 1) * LANES, :], axis=1, keepdims=True)
            flat[row + b : row + b + 1, :] = jnp.sum(
                jnp.where(sub == lane, col, 0.0), axis=0, keepdims=True
            )
        for d in range(n):
            msg_ref[d, cap : cap + share, :] = flat[d * share : (d + 1) * share, :].astype(BF16)


def reduce_kernel(cap, share, recv_ref, out_ref):
    total = recv_ref[0, cap : cap + share, :].astype(F32)
    for d in range(1, recv_ref.shape[0]):
        total = total + recv_ref[d, cap : cap + share, :].astype(F32)
    out_ref[...] = jnp.broadcast_to(total.astype(BF16)[None], out_ref.shape)


def hub_kernel(cap, recv_ref, place_ref, out_ref):
    n, width = recv_ref.shape[0], recv_ref.shape[2]
    rows = recv_ref[:, 0:cap, :].astype(F32).reshape(n * cap, width).astype(BF16)
    out_ref[...] = dot_tn(place_ref[...], rows)


def unpack_kernel(recv_ref, gws_ref, gwn_ref, gb_ref, gwc_ref, flat):
    n, share = recv_ref.shape[0], recv_ref.shape[1]
    for d in range(n):
        flat[d * share : (d + 1) * share, :] = recv_ref[d].astype(F32)
    width, hidden_rows = gws_ref.shape
    classes = gwc_ref.shape[1]
    class_rows = -(-classes // 16) * 16
    row = 0
    for b in range(hidden_rows // LANES):
        at = slice(b * LANES, (b + 1) * LANES)
        gws_ref[:, at] = flat[row : row + width, :]
        gwn_ref[:, at] = flat[row + width : row + 2 * width, :]
        row += 2 * width
    for b in range(hidden_rows // LANES):
        turned = flat[row : row + class_rows, :].T
        gwc_ref[b * LANES : (b + 1) * LANES, :] = turned[:, 0:classes]
        row += class_rows
    gb_ref[...] = flat[row : row + hidden_rows // LANES, :]


def exchange(x):
    return lax.all_to_all(x, "dom", split_axis=0, concat_axis=0, tiled=True)


def on_device(
    feats, adj_vals, adj_cols, hub_feats, hub_mirrors, hub_links, labels, groups, train_mask,
    w_self, w_neigh, bias, w_cls, group_logw,
):
    verts, width = feats.shape
    n = lax.axis_size("dom")
    hub_dev = hub_feats.shape[0]
    mirrors = hub_mirrors.shape[1]
    links = hub_links.shape[2]
    group_total = group_logw.shape[0]
    hidden_rows, classes = w_cls.shape
    class_rows = -(-classes // 16) * 16
    row_blocks, tiles = adj_cols.shape
    cap = min(hub_dev, max(2, 2 * hub_dev * mirrors // n))
    slots = n * cap
    any_space = pl.BlockSpec(memory_space=pltpu.VMEM)
    smem = pl.BlockSpec(memory_space=pltpu.SMEM)
    sds = jax.ShapeDtypeStruct

    me = lax.axis_index("dom").reshape(1).astype(I32)
    packed, place = pl.pallas_call(
        functools.partial(pack_kernel, n, cap),
        name="pack",
        out_shape=(sds((n, cap + 2 * links, width), BF16), sds((slots, hub_dev), BF16)),
        in_specs=[smem, any_space, any_space, any_space],
        out_specs=(any_space, any_space),
        compiler_params=params(),
    )(me, hub_feats, hub_mirrors.T, hub_links.transpose(1, 2, 0))
    recv = exchange(packed)

    per_step = 4
    span = per_step * LANES
    steps = row_blocks // per_step
    cols_at = lambda i, *_: (0, i)
    s_turned, f_turned, mass = pl.pallas_call(
        functools.partial(local_kernel, tiles),
        name="local",
        grid_spec=pltpu.PrefetchScalarGridSpec(
            num_scalar_prefetch=1,
            grid=(steps,),
            in_specs=[
                pl.BlockSpec((verts, width), lambda i, *_: (0, 0)),
                pl.BlockSpec((per_step, tiles, LANES, LANES), lambda i, *_: (i, 0, 0, 0)),
            ],
            out_specs=[
                pl.BlockSpec((width, span), cols_at),
                pl.BlockSpec((width, span), cols_at),
                pl.BlockSpec((8, span), cols_at),
            ],
            scratch_shapes=[pltpu.VMEM((row_blocks, width + 16, LANES), BF16)],
        ),
        out_shape=(sds((width, verts), F32), sds((width, verts), BF16), sds((8, verts), F32)),
        compiler_params=params(1),
    )(adj_cols, feats, adj_vals)

    table = (verts // LANES, LANES)
    label_table, group_table = labels.reshape(table), groups.reshape(table)
    mask_table = train_mask.reshape(table)
    w_turned = jnp.concatenate([w_self, w_neigh], axis=0).T
    wc_padded = jnp.pad(w_cls, ((0, 0), (0, class_rows - classes)))
    whole = lambda *shape: pl.BlockSpec(shape, lambda i: (0,) * len(shape))
    fa, hid, pmo, counts, inv, sums = pl.pallas_call(
        functools.partial(forward_kernel, n, cap, links, classes, span),
        name="forward",
        grid=(steps,),
        in_specs=[
            whole(n, cap + 2 * links, width),
            pl.BlockSpec((width, span), cols_at),
            pl.BlockSpec((width, span), cols_at),
            pl.BlockSpec((8, span), cols_at),
            whole(*table),
            whole(*table),
            whole(*table),
            whole(hidden_rows, 2 * width),
            whole(hidden_rows, 1),
            whole(class_rows, hidden_rows),
        ],
        out_specs=[
            pl.BlockSpec((2 * width, span), cols_at),
            pl.BlockSpec((hidden_rows, span), cols_at),
            pl.BlockSpec((class_rows, span), cols_at),
            pl.BlockSpec((span, slots), lambda i: (i, 0)),
            pl.BlockSpec((8, span), cols_at),
            whole(n, 1, LANES),
        ],
        out_shape=(
            sds((2 * width, verts), BF16),
            sds((hidden_rows, verts), BF16),
            sds((class_rows, verts), F32),
            sds((verts, slots), BF16),
            sds((8, verts), F32),
            sds((n, 1, LANES), F32),
        ),
        scratch_shapes=[
            pltpu.VMEM((width + 16, slots), BF16),
            pltpu.VMEM((links, slots), I32),
            pltpu.VMEM((links, slots), I32),
            pltpu.VMEM((group_total, LANES), F32),
            pltpu.VMEM((group_total, LANES), F32),
        ],
        compiler_params=params(1),
    )(
        recv, s_turned, f_turned, mass, label_table, group_table, mask_table,
        w_turned, bias.reshape(hidden_rows, 1), wc_padded.T,
    )
    all_sums = exchange(sums)

    grad_rows = hidden_rows // LANES * (2 * width + class_rows + 1)
    share = -(-grad_rows // (8 * n)) * 8
    message, objective = pl.pallas_call(
        functools.partial(backward_kernel, n, cap, share, span),
        name="backward",
        grid=(steps,),
        in_specs=[
            whole(n, 1, LANES),
            whole(1, group_total),
            pl.BlockSpec((class_rows, span), cols_at),
            pl.BlockSpec((hidden_rows, span), cols_at),
            pl.BlockSpec((2 * width, span), cols_at),
            pl.BlockSpec((span, slots), lambda i: (i, 0)),
            pl.BlockSpec((8, span), cols_at),
            whole(*table),
            whole(hidden_rows, class_rows),
            whole(width, hidden_rows),
        ],
        out_specs=[whole(n, cap + share, LANES), smem],
        out_shape=(sds((n, cap + share, LANES), BF16), sds((1, 1), F32)),
        scratch_shapes=[
            pltpu.VMEM((group_total, LANES), F32),
            pltpu.VMEM((2 * width, hidden_rows), F32),
            pltpu.VMEM((class_rows, hidden_rows), F32),
            pltpu.VMEM((hidden_rows, LANES), F32),
            pltpu.VMEM((width, slots), F32),
            pltpu.VMEM((n * share, LANES), F32),
        ],
        compiler_params=params(1),
    )(
        all_sums, group_logw.reshape(1, group_total), pmo, hid, fa, counts, inv, group_table,
        wc_padded, w_neigh,
    )
    answer = exchange(message)

    reduced = pl.pallas_call(
        functools.partial(reduce_kernel, cap, share),
        name="reduce",
        out_shape=sds((n, share, LANES), BF16),
        in_specs=[any_space],
        out_specs=any_space,
        compiler_params=params(),
    )(answer)
    gathered = exchange(reduced)
    hub_grad = pl.pallas_call(
        functools.partial(hub_kernel, cap),
        name="hubgrad",
        out_shape=sds((hub_dev, width), F32),
        in_specs=[any_space, any_space],
        out_specs=any_space,
        compiler_params=params(),
    )(answer, place)
    grad_w_self, grad_w_neigh, grad_bias, grad_w_cls = pl.pallas_call(
        unpack_kernel,
        name="unpack",
        out_shape=(
            sds((width, hidden_rows), F32),
            sds((width, hidden_rows), F32),
            sds((hidden_rows // LANES, LANES), F32),
            sds((hidden_rows, classes), F32),
        ),
        in_specs=[any_space],
        out_specs=(any_space,) * 4,
        scratch_shapes=[pltpu.VMEM((n * share, LANES), F32)],
        compiler_params=params(),
    )(gathered)
    return (
        objective.reshape(()), grad_w_self, grad_w_neigh, grad_bias.reshape(hidden_rows),
        grad_w_cls, hub_grad,
    )


def solution(mesh):
    in_specs = (
        P("dom", None),
        P("dom", None, None, None),
        P("dom", None),
        P("dom", None),
        P("dom", None),
        P("dom", None, None),
        P("dom"),
        P("dom"),
        P("dom"),
        P(),
        P(),
        P(),
        P(),
        P(),
    )
    out_specs = (P(), P(), P(), P(), P(), P("dom", None))
    return jax.shard_map(
        on_device, mesh=mesh, in_specs=in_specs, out_specs=out_specs, check_vma=False
    )
```

time: 471 us -> 136 us (0.29); the launches traced: 463 us -> 134 us
  other arithmetic: 136 us -> 0.73 us
  waiting for transfers between devices: 90.3 us -> 12.3 us
  Pallas kernels: 0 us -> 63.3 us
  blocking collectives: 94.6 us -> 35.6 us
  matrix products: 50.4 us -> 0 us
  local copies, waits for them, and re-layouts: 59.1 us -> 11 us
  between operations: 14.7 us -> 0.69 us
  starting transfers between devices: 16.9 us -> 10.8 us
    psum x2 -> x0, blocking collectives: 94.6 us -> none  [the longest x1 53.9 us: on_device(): gsum, count_total = lax.psum((loss_local, count_local), 'dom')]
    psum x1 -> x0, waiting for transfers between devices: 90.3 us -> none  [on_device(): lax.psum((gws, gwn, gbias, gwc), 'dom')]
    add x6 -> x0, other arithmetic: 82.5 us -> none  [the longest x2 42.2 us: spread_links(): totals + jax.ops.segment_sum(source_rows, targets[:, link_index], num_seg...]
    pallas_call x0 -> x7, Pallas kernels: none -> 63.3 us  [the longest x1 21.7 us: on_device(): pl.pallas_call(functools.partial(forward_kernel, n, cap, links, classes,...]
    dot_general x9 -> x0, matrix products: 50.4 us -> none  [the longest x1 8.59 us: on_device(): gwc = jnp.dot(hidden.T, dlogits, preferred_element_type=jnp.float32)]
    gather x10 -> x0, local copies, waits for them, and re-layouts: 42 us -> none  [the longest x8 31.9 us: gather_links(): totals = totals + padded[targets[:, link_index]]]
    all_to_all x0 -> x2, blocking collectives: none -> 35.6 us  [exchange(): return lax.all_to_all(x, 'dom', split_axis=0, concat_axis=0, tiled=True)]
    scatter-add x4 -> x0, other arithmetic: 31.8 us -> none  [the longest x2 18.1 us: spread_links(): jax.ops.segment_sum(source_rows, targets[:, link_index], num_segments=dum...]
  transfers between devices with their start and end apart: 4 -> 2, of which waited for: 1 -> 1; matrix products, arithmetic and copies ran while one was open for 20% -> 6% of each run, Pallas kernels for 0% -> 11%
where the time goes in v1:
time: 136 us; the launch traced here: 134 us
  Pallas kernels  63.3 us (47%)
  blocking collectives  35.6 us (26%)
  waiting for transfers between devices  12.3 us (9%)
  local copies, waits for them, and re-layouts  11 us (8%)
  starting transfers between devices  10.8 us (8%)
    all_to_all x2, blocking collectives, exchange(): return lax.all_to_all(x, 'dom', split_axis=0, concat_axis=0, tiled=True)  35.6 us
    pallas_call x1, Pallas kernels, on_device(): pl.pallas_call(functools.partial(forward_kernel, n, cap, links, classes,...  21.7 us
    pallas_call x1, Pallas kernels, on_device(): pl.pallas_call(functools.partial(backward_kernel, n, cap, share, span), n...  19.8 us
    pallas_call x1, Pallas kernels, on_device(): pl.pallas_call(functools.partial(local_kernel, tiles), name='local', grid...  13.2 us
    all_to_all x2, waiting for transfers between devices, exchange(): return lax.all_to_all(x, 'dom', split_axis=0, concat_axis=0, tiled=True)  12.3 us
    all_to_all x2, starting transfers between devices, exchange(): return lax.all_to_all(x, 'dom', split_axis=0, concat_axis=0, tiled=True)  10.8 us
    unnamed x9, local copies, waits for them, and re-layouts  7.94 us
  transfers between devices with their start and end apart: 2, of which 1 were waited for; matrix products, arithmetic and copies ran while one was open for 6% of the time, Pallas kernels for 11%

profile of v1, /device:TPU:0, one launch (start us, length us, event | category | flops | bytes accessed | tf_op | source)
XLA Modules:
  0.0 134.5 jit_solution(12997623093164711809)
XLA Ops:
  0.6 2.4 %pack.1 = (bf16[32,48,128]{2,1,0:T(8,128)(2,1)}, bf16[1024,64]{1,0:T(8,128)(2,1)}) custom-call(s32[1]{0:T(128)} %bitcast.me_ref, bf16[64,128]{1,0:T(8,128)(2,1)} %hub_ref.1, s32[8,64]{1,0:T(8,128)} %bitcast.19, s32[8,8,64]{2,1,0:T(8,128)} %bitcast.16), custom_call_target="tpu_custom_call" | custom-call | tf_op jit(solution)/shard_map/pack/pallas_call | solution.py:316
  3.1 7.3 %all-to-all-start = ((bf16[32,48,128]{2,1,0:T(8,128)(2,1)}), bf16[32,48,128]{2,1,0:T(8,128)(2,1)S(1)}, u32[]{:S(2)}, u32[]{:S(2)}) async-start(bf16[32,48,128]{2,1,0:T(8,128)(2,1)} %get-tuple-element.23), calls=%async_computation | async-start | bytes 786432 | tf_op jit(solution)/shard_map/all_to_all | solution.py:293
  10.4 1.4 %copy.26.cols_ref = s32[48,4]{1,0:T(8,128)} copy(s32[48,4]{0,1:T(4,128)} %param.16) | data formatting | bytes 1536 | tf_op args[2]
  11.8 1.0 copy.27
  12.8 1.0 copy.28
  13.8 1.5 %copy.30.bias_ref = f32[512,1]{1,0:T(8,128)} copy(f32[512,1]{0,1:T(1,128)} %bitcast.20) | data formatting | bytes 4096 | tf_op jit(solution)/shard_map/reshape | solution.py:399
  15.4 1.1 copy.29
  16.4 0.7 fusion
  17.2 0.8 copy.31.wc_ref
  17.9 13.2 %local.1 = (f32[128,6144]{1,0:T(8,128)}, bf16[128,6144]{1,0:T(8,128)(2,1)}, f32[8,6144]{1,0:T(8,128)}) custom-call(s32[48,4]{1,0:T(8,128)} %copy.26.cols_ref, bf16[6144,128]{1,0:T(8,128)(2,1)} %feats_ref.1, bf16[48,4,128,128]{3,2,1,0:T(8,128)(2,1)} %vals_ref.1), custom_call_target="tpu_custom_call" | custom-call | tf_op jit(solution)/shard_map/local/pallas_call | solution.py:330
  31.1 0.7 maximum_bitcast_fusion.w_ref
  31.9 0.0 all-to-all-done.recv_ref
  31.9 0.0 copy-start.1
  31.9 0.7 copy-done.1
  32.6 21.7 %forward.1 = (bf16[256,6144]{1,0:T(8,128)(2,1)}, bf16[512,6144]{1,0:T(8,128)(2,1)}, f32[176,6144]{1,0:T(8,128)}, bf16[6144,1024]{1,0:T(8,128)(2,1)}, f32[8,6144]{1,0:T(8,128)}, /*index=5*/f32[32,1,128]{2,1,0:T(1,128)}) custom-call(bf16[32,48,128]{2,1,0:T(8,128)(2,1)} %copy-done.1, f32[128,6144]{1,0:T(8,128)} %get-tuple-element.24.s_ref, ...), custom_call_target="tpu_custom_call" | custom-call | tf_op jit(solution)/shard_map/forward/pallas_call | solution.py:357
  54.4 13.0 %all_to_all.20.sums_ref = f32[32,1,128]{2,1,0:T(1,128)} all-to-all(f32[32,1,128]{2,1,0:T(1,128)} %get-tuple-element.27), channel_id=1, replica_groups=mesh['dom'=32] {'dom'}, dimensions={0} | all-to-all | bytes 32768 | tf_op jit(solution)/shard_map/all_to_all | solution.py:293
  67.4 19.8 %backward.1 = (bf16[32,88,128]{2,1,0:T(8,128)(2,1)}, f32[1,1]{1,0:T(1,128)}) custom-call(f32[32,1,128]{2,1,0:T(1,128)} %all_to_all.20.sums_ref, f32[1,64]{1,0:T(1,128)} %bitcast.21, f32[176,6144]{1,0:T(8,128)} %get-tuple-element.28.pmo_ref, bf16[512,6144]{1,0:T(8,128)(2,1)} %get-tuple-element.29.hid_ref, bf16[256,6144]{1,0:T(8,128)(2,1)} %get-tuple-element.30.fa_ref, ...), custom_call_target="tpu_custom_call" | custom-call | tf_op jit(solution)/shard_map/backward/pallas_call | solution.py:405
  87.2 22.5 %all_to_all.21.recv_ref = bf16[32,88,128]{2,1,0:T(8,128)(2,1)} all-to-all(bf16[32,88,128]{2,1,0:T(8,128)(2,1)} %get-tuple-element.34), channel_id=1, replica_groups=mesh['dom'=32] {'dom'}, dimensions={0} | all-to-all | bytes 1441792 | tf_op jit(solution)/shard_map/all_to_all | solution.py:293
  109.7 2.0 %reduce.1 = bf16[32,56,128]{2,1,0:T(8,128)(2,1)} custom-call(bf16[32,88,128]{2,1,0:T(8,128)(2,1)} %all_to_all.21.recv_ref), custom_call_target="tpu_custom_call" | custom-call | tf_op jit(solution)/shard_map/reduce/pallas_call | solution.py:438
  111.7 3.5 %all-to-all-start.3 = ((bf16[32,56,128]{2,1,0:T(8,128)(2,1)}), bf16[32,56,128]{2,1,0:T(8,128)(2,1)S(1)}, u32[]{:S(2)}, u32[]{:S(2)}) async-start(bf16[32,56,128]{2,1,0:T(8,128)(2,1)} %reduce.1), calls=%async_computation.3 | async-start | bytes 917504 | tf_op jit(solution)/shard_map/all_to_all | solution.py:293
  115.3 2.0 %hubgrad.1 = f32[64,128]{1,0:T(8,128)} custom-call(bf16[32,88,128]{2,1,0:T(8,128)(2,1)} %all_to_all.21.recv_ref, bf16[1024,64]{1,0:T(8,128)(2,1)} %get-tuple-element.39.place_ref), custom_call_target="tpu_custom_call" | custom-call | tf_op jit(solution)/shard_map/hubgrad/pallas_call | solution.py:447
  117.3 12.3 %all-to-all-done.3.recv_ref = bf16[32,56,128]{2,1,0:T(8,128)(2,1)S(1)} async-done(((bf16[32,56,128]{2,1,0:T(8,128)(2,1)}), bf16[32,56,128]{2,1,0:T(8,128)(2,1)S(1)}, u32[]{:S(2)}, u32[]{:S(2)}) %all-to-all-start.3) | async-done | bytes 458784 | tf_op jit(solution)/shard_map/all_to_all | solution.py:293
  129.6 0.0 copy-start
  129.6 0.8 copy-done
  130.4 2.1 %unpack.1 = (f32[128,512]{1,0:T(8,128)}, f32[128,512]{1,0:T(8,128)}, f32[4,128]{1,0:T(4,128)}, f32[512,172]{1,0:T(8,128)}) custom-call(bf16[32,56,128]{2,1,0:T(8,128)(2,1)} %copy-done), custom_call_target="tpu_custom_call" | custom-call | tf_op jit(solution)/shard_map/unpack/pallas_call | solution.py:455
  132.5 2.0 %copy.32 = f32[512,172]{0,1:T(8,128)} copy(f32[512,172]{1,0:T(8,128)} %get-tuple-element.50) | data formatting | bytes 704512
Async XLA Ops:
  3.1 28.8 %all-to-all-start = ((bf16[32,48,128]{2,1,0:T(8,128)(2,1)}), bf16[32,48,128]{2,1,0:T(8,128)(2,1)S(1)}, u32[]{:S(2)}, u32[]{:S(2)}) async-start(bf16[32,48,128]{2,1,0:T(8,128)(2,1)} %get-tuple-element.23), calls=%async_computation | async-start | bytes 786432 | tf_op jit(solution)/shard_map/all_to_all | solution.py:293
  31.9 0.8 copy-start.1
  111.7 17.9 %all-to-all-start.3 = ((bf16[32,56,128]{2,1,0:T(8,128)(2,1)}), bf16[32,56,128]{2,1,0:T(8,128)(2,1)S(1)}, u32[]{:S(2)}, u32[]{:S(2)}) async-start(bf16[32,56,128]{2,1,0:T(8,128)(2,1)} %reduce.1), calls=%async_computation.3 | async-start | bytes 917504 | tf_op jit(solution)/shard_map/all_to_all | solution.py:293
  129.6 0.8 copy-start

commit v2 on v1

v2 whole, which is shorter than its diff:
```python
import functools

import jax
import jax.numpy as jnp
from jax import lax
from jax.experimental import pallas as pl
from jax.experimental.pallas import tpu as pltpu
from jax.sharding import PartitionSpec as P

drift_rate = 0.5
LANES = 128
F32 = jnp.float32
BF16 = jnp.bfloat16
I32 = jnp.int32


def dot_nn(a, b):
    return lax.dot_general(a, b, (((1,), (0,)), ((), ())), preferred_element_type=F32)


def dot_nt(a, b):
    return lax.dot_general(a, b, (((1,), (1,)), ((), ())), preferred_element_type=F32)


def dot_tn(a, b):
    return lax.dot_general(a, b, (((0,), (0,)), ((), ())), preferred_element_type=F32)


def iota(shape, dim):
    return lax.broadcasted_iota(I32, shape, dim)


on_chip = pltpu.VMEM


def keep(x):
    return pltpu.with_memory_space_constraint(x, pltpu.VMEM)


def off_chip(x):
    return pltpu.with_memory_space_constraint(x, pltpu.HBM)


def params(n_grid=0, mib=20):
    kw = {} if n_grid == 0 else {"dimension_semantics": ("arbitrary",) * n_grid}
    return pltpu.CompilerParams(vmem_limit_bytes=mib << 20, **kw)


def pack_kernel(n, cap, me_ref, hub_ref, mir_ref, link_ref, out_ref, place_ref):
    hubs, width = hub_ref.shape
    mirrors, links = link_ref.shape[0], link_ref.shape[1]
    dest = iota((n, hubs), 0)
    present = jnp.zeros((n, hubs), F32)
    for j in range(mirrors):
        present = present + jnp.where(mir_ref[j : j + 1, :] == dest, 1.0, 0.0)
    before = jnp.where(iota((hubs, hubs), 0) < iota((hubs, hubs), 1), 1.0, 0.0)
    rank = dot_nn(present.astype(BF16), before.astype(BF16))
    rank = jnp.where(present > 0.0, rank, 9999.0).astype(I32)
    place = jnp.where(rank[:, None, :] == iota((n, cap, hubs), 1), 1.0, 0.0)
    place = place.reshape(n * cap, hubs).astype(BF16)
    place_ref[...] = place
    rows = dot_nn(place, hub_ref[...])
    out_ref[:, 0:cap, :] = rows.reshape(n, cap, width).astype(BF16)
    dest3 = iota((n, links, hubs), 0)
    ends = jnp.zeros((n, links, hubs), I32)
    for j in range(mirrors):
        ends = ends + jnp.where(mir_ref[j : j + 1, :][None] == dest3, link_ref[j][None], 0)
    high = ((ends >> 7) + 1).astype(F32)
    low = (ends & 127).astype(F32)
    both = jnp.concatenate([high, low], axis=1).astype(BF16)
    offset = (me_ref[0] * cap) % LANES
    lane_of = rank[:, None, :] + offset == iota((n, LANES, hubs), 1)
    lane_of = jnp.where(lane_of, 1.0, 0.0).astype(BF16)
    packed = lax.dot_general(
        both, lane_of, (((2,), (2,)), ((0,), (0,))), preferred_element_type=F32
    )
    out_ref[:, cap : cap + 2 * links, :] = packed.astype(BF16)


def to_row(block):
    eye = iota(block.shape, 0) == iota(block.shape, 1)
    return jnp.sum(jnp.where(eye, block, 0.0), axis=0, keepdims=True)


def to_column(row):
    eye = iota((LANES, LANES), 0) == iota((LANES, LANES), 1)
    return jnp.sum(jnp.where(eye, row, 0.0), axis=1, keepdims=True)


def turn(x):
    return x.astype(F32).T


def local_kernel(
    tiles, cols_ref, feats_ref, vals_ref, ws_ref, wn_ref, wc_ref, bias_ref,
    s_ref, ft_ref, mass_ref, w_ref, wct_ref, wcn_ref, biasb_ref, wide,
):
    step = pl.program_id(0)
    width = feats_ref.shape[1]
    blocks = wide.shape[0]
    hidden_rows = ws_ref.shape[1]
    classes = wc_ref.shape[0]
    class_rows = wct_ref.shape[0]

    @pl.when(step == 0)
    def _():
        def fill(b, carry):
            wide[b, :, 0:width] = feats_ref[pl.ds(pl.multiple_of(b * LANES, LANES), LANES), :]
            wide[b, :, width:] = jnp.ones((LANES, LANES), BF16)
            return carry

        lax.fori_loop(0, blocks, fill, 0, unroll=4)
        wct_ref[...] = jnp.zeros_like(wct_ref)
        wct_ref[0:classes, :] = wc_ref[...]
        for b in range(hidden_rows // LANES):
            at = slice(b * LANES, (b + 1) * LANES)
            w_ref[at, 0:width] = turn(ws_ref[:, at]).astype(BF16)
            w_ref[at, width:] = turn(wn_ref[:, at]).astype(BF16)
            wcn_ref[at, :] = turn(wct_ref[:, at]).astype(BF16)
            biasb_ref[at, :] = jnp.broadcast_to(to_column(bias_ref[b : b + 1, :]), (LANES, LANES))

    per_step = vals_ref.shape[0]
    parts = s_ref.shape[1] // LANES
    for r in range(per_step):
        block = step * per_step + r
        home, part = step * (per_step // parts) + r // parts, r % parts
        span = slice(part * LANES, (part + 1) * LANES)
        left = jnp.concatenate([vals_ref[r, k] for k in range(tiles)], axis=1)
        right = jnp.concatenate([wide[cols_ref[k, block]] for k in range(tiles)], axis=0)
        both = dot_nn(left, right)
        own = wide[block, :, 0:width].astype(F32)
        s_ref[r // parts, span, :] = own + both[:, 0:width]
        ft_ref[home, :, span] = own.T.astype(BF16)
        mass_ref[home, :, span] = to_row(both[:, width : width + LANES])


def lane_row(ref, step, parts):
    return jnp.concatenate([ref[pl.ds(step * parts + k, 1), :] for k in range(parts)], axis=1)


def fold_lanes(x):
    total = x[:, 0:LANES]
    for k in range(1, x.shape[1] // LANES):
        total = total + x[:, k * LANES : (k + 1) * LANES]
    return total


def forward_kernel(
    n, cap, links, classes, span,
    recv_ref, s_ref, ft_ref, mass_ref, label_ref, group_ref, mask_ref, w_ref, bias_ref, wc_ref,
    agg_ref, hid_ref, pmo_ref, m_ref, inv_ref, of_ref, sums_ref,
    src, word_of, value_of, loss_acc, count_acc,
):
    step = pl.program_id(0)
    slots = n * cap
    width = s_ref.shape[2]
    groups = loss_acc.shape[0]
    parts = span // LANES

    @pl.when(step == 0)
    def _():
        loss_acc[...] = jnp.zeros_like(loss_acc)
        count_acc[...] = jnp.zeros_like(count_acc)
        per = LANES // cap
        for b in range(slots // LANES):
            at = slice(b * LANES, (b + 1) * LANES)
            rows = recv_ref[b * per : (b + 1) * per, 0:cap, :].astype(F32).reshape(LANES, width)
            src[at, 0:width] = rows.astype(BF16)
            ends = recv_ref[b * per, cap : cap + 2 * links, :].astype(F32)
            for k in range(1, per):
                ends = ends + recv_ref[b * per + k, cap : cap + 2 * links, :].astype(F32)
            target = ((ends[0:links] - 1.0) * 128.0 + ends[links:]).astype(I32)
            word_of[:, at] = target >> 3
            value_of[:, at] = jnp.left_shift(1, (target & 7) * 4)
        src[:, width:] = jnp.ones((slots, LANES), BF16)

    chunk = 256
    for b in range(parts):
        first = (step * span + b * LANES) // 8
        for c in range(slots // chunk):
            at = slice(c * chunk, (c + 1) * chunk)
            rows16 = iota((16, chunk), 0) + first
            words = jnp.zeros((16, chunk), I32)
            for k in range(links):
                words = words + jnp.where(
                    word_of[k : k + 1, at] == rows16, value_of[k : k + 1, at], 0
                )
            wide = jnp.broadcast_to(words[:, None, :], (16, 8, chunk))
            count = (wide >> (4 * iota((16, 8, chunk), 1))) & 15
            m_ref[0, b * LANES : (b + 1) * LANES, at] = (
                count.reshape(LANES, chunk).astype(F32).astype(BF16)
            )
    hub = dot_nn(m_ref[0], src[...])
    total = s_ref[0] + hub[:, 0:width]
    for b in range(parts):
        at = slice(b * LANES, (b + 1) * LANES)
        inverse = 1.0 / (1.0 + mass_ref[step, :, at] + to_row(hub[at, width : width + LANES]))
        inv_ref[step, :, at] = inverse
        agg_ref[step, :, at] = (total[at, :].T * inverse).astype(BF16)
    bias = jnp.concatenate([bias_ref[...]] * parts, axis=1)
    both = jnp.concatenate([ft_ref[step], agg_ref[step]], axis=0)
    pre = dot_nn(w_ref[...], both) + bias
    hidden = jnp.maximum(pre, 0.0).astype(BF16)
    hid_ref[step] = hidden
    logits = dot_nn(wc_ref[...], hidden)
    class_row = iota(logits.shape, 0)
    logits = jnp.where(class_row < classes, logits, -jnp.inf)
    top = jnp.max(logits, axis=0, keepdims=True)
    shifted = jnp.exp(logits - top)
    total = jnp.sum(shifted, axis=0, keepdims=True)
    mask = lane_row(mask_ref, step, parts).astype(F32)
    hot = class_row == lane_row(label_ref, step, parts)
    picked = jnp.sum(jnp.where(hot, logits, 0.0), axis=0, keepdims=True)
    loss = (top + jnp.log(total) - picked) * mask
    pmo_ref[step] = mask * (shifted * (1.0 / total) - jnp.where(hot, 1.0, 0.0))
    group_row = lane_row(group_ref, step, parts)
    of_ref[step] = group_row
    in_group = iota((groups, span), 0) == group_row
    loss_acc[...] += fold_lanes(jnp.where(in_group, loss, 0.0))
    count_acc[...] += fold_lanes(jnp.where(in_group, mask, 0.0))

    @pl.when(step == pl.num_programs(0) - 1)
    def _():
        sub, lane = iota((groups, LANES), 0), iota((groups, LANES), 1)
        loss_col = jnp.sum(loss_acc[...], axis=1, keepdims=True)
        count_col = jnp.sum(count_acc[...], axis=1, keepdims=True)
        both = jnp.where(lane == sub, loss_col, 0.0) + jnp.where(
            lane == sub + groups, count_col, 0.0
        )
        row = jnp.sum(both, axis=0, keepdims=True)
        sums_ref[...] = jnp.broadcast_to(row[None], sums_ref.shape)


def backward_kernel(
    span,
    sums_ref, logw_ref, pmo_ref, hid_ref, ft_ref, agg_ref, inv_ref, group_ref, wc_ref, wn_ref,
    msg_ref, obj_ref, dsum_ref,
    q_col, gw, gwc, gb, flat,
):
    step = pl.program_id(0)
    n, share = msg_ref.shape[0], msg_ref.shape[1]
    groups = logw_ref.shape[1]
    hidden_rows = gb.shape[0]
    class_rows = pmo_ref.shape[1]

    @pl.when(step == 0)
    def _():
        row = jnp.sum(sums_ref[...], axis=0)
        sub, lane = iota((groups, LANES), 0), iota((groups, LANES), 1)
        gsum = jnp.sum(jnp.where(lane == sub, row, 0.0), axis=1, keepdims=True)
        gcount = jnp.sum(jnp.where(lane == sub + groups, row, 0.0), axis=1, keepdims=True)
        sub, lane = iota((groups, groups), 0), iota((groups, groups), 1)
        logw = jnp.sum(jnp.where(lane == sub, logw_ref[...], 0.0), axis=1, keepdims=True)
        score = logw + drift_rate * gsum / (gcount + 1.0)
        e = jnp.exp(score - jnp.max(score, axis=0, keepdims=True))
        q = groups * (e / jnp.sum(e, axis=0, keepdims=True))
        obj_ref[0, 0] = jnp.sum(q * gsum)
        q_col[...] = jnp.broadcast_to(q, q_col.shape)
        gw[...] = jnp.zeros_like(gw)
        gwc[...] = jnp.zeros_like(gwc)
        gb[...] = jnp.zeros_like(gb)

    in_group = iota((groups, span), 0) == group_ref[step]
    weight = jnp.sum(jnp.where(in_group, q_col[:, 0:1], 0.0), axis=0, keepdims=True)
    dlogits = (pmo_ref[step] * weight).astype(BF16)
    hidden = hid_ref[step]
    gwc[...] += dot_nt(hidden, dlogits)
    dhidden = dot_nn(wc_ref[...], dlogits)
    dfull = jnp.where(hidden.astype(F32) > 0.0, dhidden, 0.0)
    gb[...] += fold_lanes(dfull)
    dpre = dfull.astype(BF16)
    gw[...] += dot_nt(dpre, jnp.concatenate([ft_ref[step], agg_ref[step]], axis=0))
    dagg = dot_nn(wn_ref[...], dpre)
    dsum_ref[step] = (dagg * inv_ref[step]).astype(BF16)

    @pl.when(step == pl.num_programs(0) - 1)
    def _():
        row = 0
        for b in range(gw.shape[1] // LANES):
            flat[row : row + hidden_rows, :] = gw[:, b * LANES : (b + 1) * LANES]
            row += hidden_rows
        for b in range(hidden_rows // LANES):
            flat[row : row + class_rows, :] = gwc[b * LANES : (b + 1) * LANES, :].T
            row += class_rows
        flat[row:, :] = jnp.zeros((flat.shape[0] - row, LANES), F32)
        for b in range(hidden_rows // LANES):
            col = jnp.sum(gb[b * LANES : (b + 1) * LANES, :], axis=1, keepdims=True)
            flat[row + b : row + b + 1, :] = to_row(jnp.broadcast_to(col, (LANES, LANES)))
        for d in range(n):
            msg_ref[d] = flat[d * share : (d + 1) * share, :].astype(BF16)


def slot_kernel(dsum_ref, m_ref, place_ref, out_ref, turned_ref, slot):
    step = pl.program_id(0)
    n, cap = out_ref.shape[0], out_ref.shape[1]
    slots = n * cap

    @pl.when(step == 0)
    def _():
        slot[...] = jnp.zeros_like(slot)
        for b in range(slots // LANES):
            at = slice(b * LANES, (b + 1) * LANES)
            turned_ref[:, at] = turn(place_ref[at, :]).astype(BF16)

    slot[...] += dot_nn(dsum_ref[step], m_ref[0])

    @pl.when(step == pl.num_programs(0) - 1)
    def _():
        per = LANES // cap
        for b in range(slots // LANES):
            rows = slot[:, b * LANES : (b + 1) * LANES].T
            out_ref[b * per : (b + 1) * per] = rows.reshape(per, cap, LANES).astype(BF16)


def reduce_kernel(recv_ref, slot_ref, out_ref):
    n, cap, width = slot_ref.shape
    share = recv_ref.shape[1]
    total = recv_ref[0].astype(F32)
    for d in range(1, n):
        total = total + recv_ref[d].astype(F32)
    total = total.astype(BF16)
    out_ref[:, 0:cap, :] = slot_ref[...]
    out_ref[:, cap:, :] = jnp.broadcast_to(total[None], (n, share, width))


def final_kernel(cap, recv_ref, place_ref, gws_ref, gwn_ref, gb_ref, gwc_ref, hub_ref, flat):
    n, share, width = recv_ref.shape[0], recv_ref.shape[1] - cap, recv_ref.shape[2]
    rows = recv_ref[:, 0:cap, :].astype(F32).reshape(n * cap, width).astype(BF16)
    hub_ref[...] = dot_nn(place_ref[...], rows)
    for d in range(n):
        flat[d * share : (d + 1) * share, :] = recv_ref[d, cap:, :].astype(F32)
    hidden_rows = gws_ref.shape[1]
    classes = gwc_ref.shape[0]
    class_rows = -(-classes // 16) * 16
    row = 2 * hidden_rows
    for b in range(hidden_rows // LANES):
        at = slice(b * LANES, (b + 1) * LANES)
        gws_ref[:, at] = flat[b * LANES : (b + 1) * LANES, :].T
        gwn_ref[:, at] = flat[hidden_rows + b * LANES : hidden_rows + (b + 1) * LANES, :].T
        gwc_ref[:, at] = flat[row : row + classes, :]
        row += class_rows
    gb_ref[...] = flat[row : row + hidden_rows // LANES, :]


def exchange(x):
    return lax.all_to_all(x, "dom", split_axis=0, concat_axis=0, tiled=True)


def on_device(
    feats, adj_vals, adj_cols, hub_feats, hub_mirrors, hub_links, labels, groups, train_mask,
    w_self, w_neigh, bias, w_cls, group_logw,
):
    verts, width = feats.shape
    n = lax.axis_size("dom")
    hub_dev = hub_feats.shape[0]
    mirrors = hub_mirrors.shape[1]
    links = hub_links.shape[2]
    group_total = group_logw.shape[0]
    hidden_rows, classes = w_cls.shape
    class_rows = -(-classes // 16) * 16
    row_blocks, tiles = adj_cols.shape
    cap = min(hub_dev, max(2, 2 * hub_dev * mirrors // n))
    slots = n * cap
    any_space = pl.BlockSpec(memory_space=pltpu.VMEM)
    smem = pl.BlockSpec(memory_space=pltpu.SMEM)
    sds = jax.ShapeDtypeStruct

    me = lax.axis_index("dom").reshape(1).astype(I32)
    packed, place = pl.pallas_call(
        functools.partial(pack_kernel, n, cap),
        name="pack",
        out_shape=(sds((n, cap + 2 * links, width), BF16), sds((slots, hub_dev), BF16)),
        in_specs=[smem, any_space, any_space, any_space],
        out_specs=(any_space, any_space),
        compiler_params=params(),
    )(me, off_chip(hub_feats), off_chip(hub_mirrors.T), off_chip(hub_links.transpose(1, 2, 0)))
    recv = exchange(packed)

    parts = 8
    span = parts * LANES
    steps = row_blocks // parts
    per_step = parts
    whole = lambda *shape: pl.BlockSpec(shape, lambda i, *_: (0,) * len(shape))
    s_rows, f_turned, mass, w_turned, wc_turned, wc_rows, bias_wide = pl.pallas_call(
        functools.partial(local_kernel, tiles),
        name="local",
        grid_spec=pltpu.PrefetchScalarGridSpec(
            num_scalar_prefetch=1,
            grid=(row_blocks // per_step,),
            in_specs=[
                whole(verts, width),
                pl.BlockSpec((per_step, tiles, LANES, LANES), lambda i, *_: (i, 0, 0, 0)),
                whole(width, hidden_rows),
                whole(width, hidden_rows),
                whole(classes, hidden_rows),
                whole(hidden_rows // LANES, LANES),
            ],
            out_specs=[
                pl.BlockSpec((per_step // parts, span, width), lambda i, *_: (i, 0, 0))
            ]
            + [any_space] * 4
            + [whole(hidden_rows, class_rows), any_space],
            scratch_shapes=[pltpu.VMEM((row_blocks, LANES, 2 * width), BF16)],
        ),
        out_shape=(
            pltpu.HBM((steps, span, width), F32),
            on_chip((steps, width, span), BF16),
            on_chip((steps, 1, span), F32),
            on_chip((hidden_rows, 2 * width), BF16),
            on_chip((class_rows, hidden_rows), BF16),
            pltpu.HBM((hidden_rows, class_rows), BF16),
            on_chip((hidden_rows, LANES), F32),
        ),
        compiler_params=params(1, 16),
    )(
        off_chip(adj_cols.T), off_chip(feats), off_chip(adj_vals), off_chip(w_self), off_chip(w_neigh),
        off_chip(w_cls.T), off_chip(bias.reshape(hidden_rows // LANES, LANES)),
    )

    table = (verts // LANES, LANES)
    label_table, group_table = keep(labels.reshape(table)), keep(groups.reshape(table))
    mask_table = keep(train_mask.reshape(table))
    tile_at = pl.BlockSpec((1, span, slots), lambda i: (i, 0, 0))
    agg, hid, pmo, counts, inv, group_rows, sums = pl.pallas_call(
        functools.partial(forward_kernel, n, cap, links, classes, span),
        name="forward",
        grid=(steps,),
        in_specs=[any_space, pl.BlockSpec((1, span, width), lambda i: (i, 0, 0))]
        + [any_space] * 8,
        out_specs=[any_space] * 3 + [tile_at] + [any_space] * 3,
        out_shape=(
            on_chip((steps, width, span), BF16),
            on_chip((steps, hidden_rows, span), BF16),
            on_chip((steps, class_rows, span), F32),
            pltpu.HBM((steps, span, slots), BF16),
            on_chip((steps, 1, span), F32),
            on_chip((steps, 1, span), I32),
            sds((n, 1, LANES), F32),
        ),
        scratch_shapes=[
            pltpu.VMEM((slots, 2 * width), BF16),
            pltpu.VMEM((links, slots), I32),
            pltpu.VMEM((links, slots), I32),
            pltpu.VMEM((group_total, LANES), F32),
            pltpu.VMEM((group_total, LANES), F32),
        ],
        compiler_params=params(1),
    )(
        keep(recv), off_chip(s_rows), keep(f_turned), keep(mass), label_table, group_table,
        mask_table, keep(w_turned), keep(bias_wide), keep(wc_turned),
    )
    all_sums = exchange(sums)

    grad_rows = hidden_rows // LANES * (2 * width + class_rows + 1)
    share = -(-grad_rows // (8 * n)) * 8
    message, objective, dsum = pl.pallas_call(
        functools.partial(backward_kernel, span),
        name="backward",
        grid=(steps,),
        in_specs=[any_space] * 10,
        out_specs=[any_space, smem, any_space],
        out_shape=(
            pltpu.HBM((n, share, LANES), BF16), sds((1, 1), F32), on_chip((steps, width, span), BF16),
        ),
        scratch_shapes=[
            pltpu.VMEM((group_total, LANES), F32),
            pltpu.VMEM((hidden_rows, 2 * width), F32),
            pltpu.VMEM((hidden_rows, class_rows), F32),
            pltpu.VMEM((hidden_rows, LANES), F32),
            pltpu.VMEM((n * share, LANES), F32),
        ],
        compiler_params=params(1),
    )(
        all_sums, group_logw.reshape(1, group_total), keep(pmo), keep(hid), keep(f_turned),
        keep(agg), keep(inv), keep(group_rows), keep(wc_rows), keep(w_neigh),
    )
    answer = exchange(message)

    slot_grads, place_turned = pl.pallas_call(
        slot_kernel,
        name="slots",
        grid=(steps,),
        in_specs=[any_space, tile_at, any_space],
        out_specs=[any_space] * 2,
        out_shape=(on_chip((n, cap, width), BF16), on_chip((hub_dev, slots), BF16)),
        scratch_shapes=[pltpu.VMEM((width, slots), F32)],
        compiler_params=params(1),
    )(keep(dsum), off_chip(counts), keep(place))
    reduced = pl.pallas_call(
        reduce_kernel,
        name="reduce",
        out_shape=sds((n, cap + share, LANES), BF16),
        in_specs=[any_space, any_space],
        out_specs=any_space,
        compiler_params=params(),
    )(keep(answer), keep(slot_grads))
    gathered = exchange(reduced)
    grad_w_self, grad_w_neigh, grad_bias, grad_w_cls, hub_grad = pl.pallas_call(
        functools.partial(final_kernel, cap),
        name="final",
        out_shape=(
            sds((width, hidden_rows), F32),
            sds((width, hidden_rows), F32),
            sds((hidden_rows // LANES, LANES), F32),
            sds((classes, hidden_rows), F32),
            sds((hub_dev, width), F32),
        ),
        in_specs=[any_space, any_space],
        out_specs=(any_space,) * 5,
        scratch_shapes=[pltpu.VMEM((n * share, LANES), F32)],
        compiler_params=params(),
    )(keep(gathered), keep(place_turned))
    return (
        objective.reshape(()), grad_w_self, grad_w_neigh, grad_bias.reshape(hidden_rows),
        grad_w_cls.T, hub_grad,
    )


def solution(mesh):
    in_specs = (
        P("dom", None),
        P("dom", None, None, None),
        P("dom", None),
        P("dom", None),
        P("dom", None),
        P("dom", None, None),
        P("dom"),
        P("dom"),
        P("dom"),
        P(),
        P(),
        P(),
        P(),
        P(),
    )
    out_specs = (P(), P(), P(), P(), P(), P("dom", None))
    return jax.shard_map(
        on_device, mesh=mesh, in_specs=in_specs, out_specs=out_specs, check_vma=False
    )
```

time: 136 us -> 101 us (0.74)
  Pallas kernels: 63.3 us -> 47.6 us
  local copies, waits for them, and re-layouts: 11 us -> 0.03 us
  blocking collectives: 35.6 us -> 31.4 us
  waiting for transfers between devices: 12.3 us -> 10.8 us
    pallas_call x4, Pallas kernels: 25.9 us -> 17.7 us  [the longest x1 9.15 us: on_device(): pl.pallas_call(functools.partial(backward_kernel, span), name='backward',...]
    unnamed x9 -> x12, local copies, waits for them, and re-layouts: 7.94 us -> 0.03 us
    all_to_all x2, blocking collectives: 35.6 us -> 31.4 us  [exchange(): return lax.all_to_all(x, 'dom', split_axis=0, concat_axis=0, tiled=True)]
    pallas_call x1, Pallas kernels: 13.2 us -> 9.33 us  [on_device(): pl.pallas_call(functools.partial(local_kernel, tiles), name='local', grid...]
    pallas_call x1, Pallas kernels: 21.7 us -> 18.2 us  [on_device(): pl.pallas_call(functools.partial(forward_kernel, n, cap, links, classes,...]
    reshape x1 -> x0, local copies, waits for them, and re-layouts: 1.54 us -> none  [on_device(): bias.reshape(hidden_rows, 1)]
    all_to_all x2, waiting for transfers between devices: 12.3 us -> 10.8 us  [exchange(): return lax.all_to_all(x, 'dom', split_axis=0, concat_axis=0, tiled=True)]
  transfers between devices with their start and end apart: 2 -> 2, of which waited for: 1 -> 2; matrix products, arithmetic and copies ran while one was open for 6% -> 0% of each run, Pallas kernels for 11% -> 17%
where the time goes in v2:
time: 101 us; the launch traced here: 100 us
  Pallas kernels  47.6 us (47%)
  blocking collectives  31.4 us (31%)
  waiting for transfers between devices  10.8 us (11%)
  starting transfers between devices  9.91 us (10%)
    all_to_all x2, blocking collectives, exchange(): return lax.all_to_all(x, 'dom', split_axis=0, concat_axis=0, tiled=True)  31.4 us
    pallas_call x1, Pallas kernels, on_device(): pl.pallas_call(functools.partial(forward_kernel, n, cap, links, classes,...  18.2 us
    all_to_all x2, waiting for transfers between devices, exchange(): return lax.all_to_all(x, 'dom', split_axis=0, concat_axis=0, tiled=True)  10.8 us
    all_to_all x2, starting transfers between devices, exchange(): return lax.all_to_all(x, 'dom', split_axis=0, concat_axis=0, tiled=True)  9.91 us
    pallas_call x1, Pallas kernels, on_device(): pl.pallas_call(functools.partial(local_kernel, tiles), name='local', grid...  9.33 us
    pallas_call x1, Pallas kernels, on_device(): pl.pallas_call(functools.partial(backward_kernel, span), name='backward',...  9.15 us
    pallas_call x1, Pallas kernels, on_device(): pl.pallas_call(slot_kernel, name='slots', grid=(steps,), in_specs=[any_sp...  7.35 us
    pallas_call x1, Pallas kernels, on_device(): pl.pallas_call(functools.partial(pack_kernel, n, cap), name='pack', out_s...  2.44 us
  transfers between devices with their start and end apart: 2, of which 2 were waited for; matrix products, arithmetic and copies ran while one was open for 0% of the time, Pallas kernels for 17%

profile of v2, /device:TPU:0, one launch (start us, length us, event | category | flops | bytes accessed | tf_op | source)
XLA Modules:
  0.0 100.5 jit_solution(10401534189907516080)
XLA Ops:
  0.6 2.4 %pack.1 = (bf16[32,48,128]{2,1,0:T(8,128)(2,1)}, bf16[1024,64]{1,0:T(8,128)(2,1)S(1)}) custom-call(s32[1]{0:T(128)} %bitcast.me_ref, bf16[64,128]{1,0:T(8,128)(2,1)} %hub_ref.1, s32[8,64]{1,0:T(8,128)} %bitcast.19, s32[8,8,64]{2,1,0:T(8,128)} %bitcast.18), custom_call_target="tpu_custom_call" | custom-call | tf_op jit(solution)/shard_map/pack/pallas_call | solution.py:369
  3.1 7.3 %all-to-all-start = ((bf16[32,48,128]{2,1,0:T(8,128)(2,1)}), bf16[32,48,128]{2,1,0:T(8,128)(2,1)S(1)}, u32[]{:S(2)}, u32[]{:S(2)}) async-start(bf16[32,48,128]{2,1,0:T(8,128)(2,1)} %get-tuple-element.32), calls=%async_computation | async-start | bytes 786432 | tf_op jit(solution)/shard_map/all_to_all | solution.py:346
  10.4 0.0 copy-start.2
  10.4 0.0 copy-start.3
  10.4 0.0 copy-start.4
  10.4 9.3 %local.1 = (f32[6,1024,128]{2,1,0:T(8,128)}, bf16[6,128,1024]{2,1,0:T(8,128)(2,1)S(1)}, f32[6,1,1024]{2,1,0:T(1,128)S(1)}, bf16[512,256]{1,0:T(8,128)(2,1)S(1)},...) custom-call(s32[4,48]{1,0:T(4,128)} %bitcast.20, bf16[6144,128]{1,0:T(8,128)(2,1)} %feats_ref.1, ...), custom_call_target="tpu_custom_call" | custom-call | tf_op jit(solution)/shard_map/local/pallas_call | solution.py:384
  19.7 0.0 copy-start
  19.7 0.0 copy-start.5
  19.7 3.8 %all-to-all-done.recv_ref = bf16[32,48,128]{2,1,0:T(8,128)(2,1)S(1)} async-done(((bf16[32,48,128]{2,1,0:T(8,128)(2,1)}), bf16[32,48,128]{2,1,0:T(8,128)(2,1)S(1)}, u32[]{:S(2)}, u32[]{:S(2)}) %all-to-all-start) | async-done | bytes 393248 | tf_op jit(solution)/shard_map/all_to_all | solution.py:346
  23.6 0.0 copy-start.1
  23.6 0.0 copy-done.2
  23.6 0.0 copy-done.3
  23.6 0.0 copy-done.4
  23.6 18.2 %forward.1 = (bf16[6,128,1024]{2,1,0:T(8,128)(2,1)S(1)}, bf16[6,512,1024]{2,1,0:T(8,128)(2,1)S(1)}, f32[6,176,1024]{2,1,0:T(8,128)S(1)}, bf16[6,1024,1024]{2,1,0...) custom-call(bf16[32,48,128]{2,1,0:T(8,128)(2,1)S(1)} %all-to-all-done.recv_ref, ...), custom_call_target="tpu_custom_call" | custom-call | tf_op jit(solution)/shard_map/forward/pallas_call | solution.py:424
  41.8 9.6 %all_to_all.20.sums_ref = f32[32,1,128]{2,1,0:T(1,128)S(1)} all-to-all(f32[32,1,128]{2,1,0:T(1,128)S(1)} %get-tuple-element.39), channel_id=1, replica_groups=mesh['dom'=32] {'dom'}, dimensions={0} | all-to-all | bytes 32768 | tf_op jit(solution)/shard_map/all_to_all | solution.py:346
  51.4 0.0 copy-done
  51.4 0.0 copy-done.5
  51.4 0.0 copy-done.1
  51.4 9.1 %backward.1 = (bf16[32,56,128]{2,1,0:T(8,128)(2,1)}, f32[1,1]{1,0:T(1,128)}, bf16[6,128,1024]{2,1,0:T(8,128)(2,1)S(1)}) custom-call(f32[32,1,128]{2,1,0:T(1,128)S(1)} %all_to_all.20.sums_ref, f32[1,64]{1,0:T(1,128)S(1)} %bitcast.16, f32[6,176,1024]{2,1,0:T(8,128)S(1)} %get-tuple-element.40.pmo_ref, bf16[6,512,1024]{2,1,0:T(8,128)(2,1)S(1)} %get-tuple-element.41.hid_ref, ...), custom_call_target="tpu_custom_call" | custom-call | tf_op jit(solution)/shard_map/backward/pallas_call | solution.py:456
  60.5 2.6 %all-to-all-start.2 = ((bf16[32,56,128]{2,1,0:T(8,128)(2,1)}), bf16[32,56,128]{2,1,0:T(8,128)(2,1)S(1)}, u32[]{:S(2)}, u32[]{:S(2)}) async-start(bf16[32,56,128]{2,1,0:T(8,128)(2,1)} %get-tuple-element.47), calls=%async_computation.2 | async-start | bytes 917504 | tf_op jit(solution)/shard_map/all_to_all | solution.py:346
  63.1 7.3 %slots.1 = (bf16[32,32,128]{2,1,0:T(8,128)(2,1)S(1)}, bf16[64,1024]{1,0:T(8,128)(2,1)S(1)}) custom-call(bf16[6,128,1024]{2,1,0:T(8,128)(2,1)S(1)} %get-tuple-element.48.dsum_ref, bf16[6,1024,1024]{2,1,0:T(8,128)(2,1)} %get-tuple-element.49.m_ref, bf16[1024,64]{1,0:T(8,128)(2,1)S(1)} %get-tuple-element.50.place_ref), custom_call_target="tpu_custom_call" | custom-call | tf_op jit(solution)/shard_map/slots/pallas_call | solution.py:479
  70.5 7.0 %all-to-all-done.2.recv_ref = bf16[32,56,128]{2,1,0:T(8,128)(2,1)S(1)} async-done(((bf16[32,56,128]{2,1,0:T(8,128)(2,1)}), bf16[32,56,128]{2,1,0:T(8,128)(2,1)S(1)}, u32[]{:S(2)}, u32[]{:S(2)}) %all-to-all-start.2) | async-done | bytes 458784 | tf_op jit(solution)/shard_map/all_to_all | solution.py:346
  77.5 0.1 reduce.1
  77.6 21.8 %all_to_all.21.recv_ref = bf16[32,88,128]{2,1,0:T(8,128)(2,1)S(1)} all-to-all(bf16[32,88,128]{2,1,0:T(8,128)(2,1)S(1)} %reduce.1), channel_id=1, replica_groups=mesh['dom'=32] {'dom'}, dimensions={0} | all-to-all | bytes 1441792 | tf_op jit(solution)/shard_map/all_to_all | solution.py:346
  99.4 1.1 %final.1 = (f32[128,512]{1,0:T(8,128)}, f32[128,512]{1,0:T(8,128)}, f32[4,128]{1,0:T(4,128)}, f32[172,512]{1,0:T(8,128)}, f32[64,128]{1,0:T(8,128)}) custom-call(bf16[32,88,128]{2,1,0:T(8,128)(2,1)S(1)} %all_to_all.21.recv_ref, bf16[64,1024]{1,0:T(8,128)(2,1)S(1)} %get-tuple-element.52.place_ref), custom_call_target="tpu_custom_call" | custom-call | tf_op jit(solution)/shard_map/final/pallas_call | solution.py:498
Async XLA Ops:
  3.1 20.5 %all-to-all-start = ((bf16[32,48,128]{2,1,0:T(8,128)(2,1)}), bf16[32,48,128]{2,1,0:T(8,128)(2,1)S(1)}, u32[]{:S(2)}, u32[]{:S(2)}) async-start(bf16[32,48,128]{2,1,0:T(8,128)(2,1)} %get-tuple-element.32), calls=%async_computation | async-start | bytes 786432 | tf_op jit(solution)/shard_map/all_to_all | solution.py:346
  10.4 13.2 %copy-start.2 = (s32[6144]{0:T(1024)S(1)}, s32[6144]{0:T(1024)}, u32[]{:S(2)}) copy-start(s32[6144]{0:T(1024)} %param.20) | copy-start | bytes 73732
  10.4 13.2 %copy-start.3 = (s32[6144]{0:T(1024)S(1)}, s32[6144]{0:T(1024)}, u32[]{:S(2)}) copy-start(s32[6144]{0:T(1024)} %param.21) | copy-start | bytes 73732
  10.4 13.2 %copy-start.4 = (s32[6144]{0:T(1024)S(1)}, s32[6144]{0:T(1024)}, u32[]{:S(2)}) copy-start(s32[6144]{0:T(1024)} %param.22) | copy-start | bytes 73732
  19.7 31.6 %copy-start = (bf16[128,512]{1,0:T(8,128)(2,1)S(1)}, bf16[128,512]{1,0:T(8,128)(2,1)}, u32[]{:S(2)}) copy-start(bf16[128,512]{1,0:T(8,128)(2,1)} %wn_ref.3) | copy-start | bytes 393220
  19.7 31.6 %copy-start.5 = (f32[64]{0:T(128)S(1)}, f32[64]{0:T(128)}, u32[]{:S(2)}) copy-start(f32[64]{0:T(128)} %param.27) | copy-start | bytes 772
  23.6 27.8 %copy-start.1 = (bf16[512,176]{1,0:T(8,128)(2,1)S(1)}, bf16[512,176]{1,0:T(8,128)(2,1)}, u32[]{:S(2)}) copy-start(bf16[512,176]{1,0:T(8,128)(2,1)} %get-tuple-element.45.wc_ref) | copy-start | bytes 540676
  60.5 17.0 %all-to-all-start.2 = ((bf16[32,56,128]{2,1,0:T(8,128)(2,1)}), bf16[32,56,128]{2,1,0:T(8,128)(2,1)S(1)}, u32[]{:S(2)}, u32[]{:S(2)}) async-start(bf16[32,56,128]{2,1,0:T(8,128)(2,1)} %get-tuple-element.47), calls=%async_computation.2 | async-start | bytes 917504 | tf_op jit(solution)/shard_map/all_to_all | solution.py:346

commit v3 on v2

--- a/solution.py
+++ b/solution.py
@@ -46,7 +46,7 @@
     return pltpu.CompilerParams(vmem_limit_bytes=mib << 20, **kw)
 
 
-def pack_kernel(n, cap, me_ref, hub_ref, mir_ref, link_ref, out_ref, place_ref):
+def pack_kernel(n, cap, hub_ref, mir_ref, link_ref, out_ref, place_ref):
     hubs, width = hub_ref.shape
     mirrors, links = link_ref.shape[0], link_ref.shape[1]
     dest = iota((n, hubs), 0)
@@ -57,9 +57,9 @@
     rank = dot_nn(present.astype(BF16), before.astype(BF16))
     rank = jnp.where(present > 0.0, rank, 9999.0).astype(I32)
     place = jnp.where(rank[:, None, :] == iota((n, cap, hubs), 1), 1.0, 0.0)
-    place = place.reshape(n * cap, hubs).astype(BF16)
-    place_ref[...] = place
-    rows = dot_nn(place, hub_ref[...])
+    flat_place = place.reshape(n * cap, hubs).astype(BF16)
+    place_ref[...] = flat_place
+    rows = dot_nn(flat_place, hub_ref[...])
     out_ref[:, 0:cap, :] = rows.reshape(n, cap, width).astype(BF16)
     dest3 = iota((n, links, hubs), 0)
     ends = jnp.zeros((n, links, hubs), I32)
@@ -68,13 +68,12 @@
     high = ((ends >> 7) + 1).astype(F32)
     low = (ends & 127).astype(F32)
     both = jnp.concatenate([high, low], axis=1).astype(BF16)
-    offset = (me_ref[0] * cap) % LANES
-    lane_of = rank[:, None, :] + offset == iota((n, LANES, hubs), 1)
-    lane_of = jnp.where(lane_of, 1.0, 0.0).astype(BF16)
     packed = lax.dot_general(
-        both, lane_of, (((2,), (2,)), ((0,), (0,))), preferred_element_type=F32
-    )
-    out_ref[:, cap : cap + 2 * links, :] = packed.astype(BF16)
+        both, place.astype(BF16), (((2,), (2,)), ((0,), (0,))), preferred_element_type=F32
+    )
+    rows = 2 * links * cap // LANES
+    lanes = [packed[:, q * rows : (q + 1) * rows, :] for q in range(LANES // cap)]
+    out_ref[:, cap : cap + rows, :] = jnp.concatenate(lanes, axis=2).astype(BF16)
 
 
 def to_row(block):
@@ -120,7 +119,7 @@
             biasb_ref[at, :] = jnp.broadcast_to(to_column(bias_ref[b : b + 1, :]), (LANES, LANES))
 
     per_step = vals_ref.shape[0]
-    parts = s_ref.shape[1] // LANES
+    parts = s_ref.shape[2] // LANES
     for r in range(per_step):
         block = step * per_step + r
         home, part = step * (per_step // parts) + r // parts, r % parts
@@ -128,9 +127,9 @@
         left = jnp.concatenate([vals_ref[r, k] for k in range(tiles)], axis=1)
         right = jnp.concatenate([wide[cols_ref[k, block]] for k in range(tiles)], axis=0)
         both = dot_nn(left, right)
-        own = wide[block, :, 0:width].astype(F32)
-        s_ref[r // parts, span, :] = own + both[:, 0:width]
-        ft_ref[home, :, span] = own.T.astype(BF16)
+        own = wide[block, :, 0:width].astype(F32).T
+        s_ref[r // parts, :, span] = own + both[:, 0:width].T
+        ft_ref[home, :, span] = own.astype(BF16)
         mass_ref[home, :, span] = to_row(both[:, width : width + LANES])
 
 
@@ -153,7 +152,7 @@
 ):
     step = pl.program_id(0)
     slots = n * cap
-    width = s_ref.shape[2]
+    width = s_ref.shape[1]
     groups = loss_acc.shape[0]
     parts = span // LANES
 
@@ -162,41 +161,45 @@
         loss_acc[...] = jnp.zeros_like(loss_acc)
         count_acc[...] = jnp.zeros_like(count_acc)
         per = LANES // cap
+        rows = 2 * links // per
+        block_of = iota((1, 1, LANES), 2) // cap
+        ends = recv_ref[:, cap : cap + rows, :].astype(F32).reshape(n // per, per, rows, LANES)
+        ends = [ends[:, k] for k in range(per)]
+        turned = [[pltpu.roll(e, t * cap, 2) if t else e for t in range(per)] for e in ends]
+        values = []
+        for q in range(per):
+            value = jnp.zeros((n // per, rows, LANES), F32)
+            for k in range(per):
+                value = jnp.where(block_of == k, turned[k][(k - q) % per], value)
+            values.append(value)
+        ends = jnp.concatenate(values, axis=1)
         for b in range(slots // LANES):
             at = slice(b * LANES, (b + 1) * LANES)
             rows = recv_ref[b * per : (b + 1) * per, 0:cap, :].astype(F32).reshape(LANES, width)
-            src[at, 0:width] = rows.astype(BF16)
-            ends = recv_ref[b * per, cap : cap + 2 * links, :].astype(F32)
-            for k in range(1, per):
-                ends = ends + recv_ref[b * per + k, cap : cap + 2 * links, :].astype(F32)
-            target = ((ends[0:links] - 1.0) * 128.0 + ends[links:]).astype(I32)
-            word_of[:, at] = target >> 3
-            value_of[:, at] = jnp.left_shift(1, (target & 7) * 4)
-        src[:, width:] = jnp.ones((slots, LANES), BF16)
+            src[0:width, at] = rows.T.astype(BF16)
+            target = ((ends[b, 0:links] - 1.0) * 128.0 + ends[b, links:]).astype(I32)
+            word_of[:, at] = (target >> 7) * 16 + (target & 15)
+            value_of[:, at] = jnp.left_shift(1, ((target >> 4) & 7) * 4)
+        src[width:, :] = jnp.ones((16, slots), BF16)
 
     chunk = 256
-    for b in range(parts):
-        first = (step * span + b * LANES) // 8
-        for c in range(slots // chunk):
-            at = slice(c * chunk, (c + 1) * chunk)
-            rows16 = iota((16, chunk), 0) + first
-            words = jnp.zeros((16, chunk), I32)
+    for c in range(slots // chunk):
+        at = slice(c * chunk, (c + 1) * chunk)
+        word = [jnp.broadcast_to(word_of[k : k + 1, at], (16, chunk)) for k in range(links)]
+        value = [jnp.broadcast_to(value_of[k : k + 1, at], (16, chunk)) for k in range(links)]
+        for b in range(parts):
+            rows16 = iota((16, chunk), 0) + (step * parts + b) * 16
+            fields = jnp.zeros((16, chunk), I32)
             for k in range(links):
-                words = words + jnp.where(
-                    word_of[k : k + 1, at] == rows16, value_of[k : k + 1, at], 0
-                )
-            wide = jnp.broadcast_to(words[:, None, :], (16, 8, chunk))
-            count = (wide >> (4 * iota((16, 8, chunk), 1))) & 15
-            m_ref[0, b * LANES : (b + 1) * LANES, at] = (
-                count.reshape(LANES, chunk).astype(F32).astype(BF16)
-            )
-    hub = dot_nn(m_ref[0], src[...])
-    total = s_ref[0] + hub[:, 0:width]
-    for b in range(parts):
-        at = slice(b * LANES, (b + 1) * LANES)
-        inverse = 1.0 / (1.0 + mass_ref[step, :, at] + to_row(hub[at, width : width + LANES]))
-        inv_ref[step, :, at] = inverse
-        agg_ref[step, :, at] = (total[at, :].T * inverse).astype(BF16)
+                fields = fields + jnp.where(word[k] == rows16, value[k], 0)
+            for f in range(8):
+                first = b * LANES + f * 16
+                count = (fields >> (4 * f)) & 15
+                m_ref[0, first : first + 16, at] = count.astype(F32).astype(BF16)
+    hub = dot_nt(src[...], m_ref[0])
+    inverse = 1.0 / (1.0 + mass_ref[step] + hub[width : width + 1, :])
+    inv_ref[step] = inverse
+    agg_ref[step] = ((s_ref[0] + hub[0:width]) * inverse).astype(BF16)
     bias = jnp.concatenate([bias_ref[...]] * parts, axis=1)
     both = jnp.concatenate([ft_ref[step], agg_ref[step]], axis=0)
     pre = dot_nn(w_ref[...], both) + bias
@@ -266,9 +269,9 @@
     hidden = hid_ref[step]
     gwc[...] += dot_nt(hidden, dlogits)
     dhidden = dot_nn(wc_ref[...], dlogits)
-    dfull = jnp.where(hidden.astype(F32) > 0.0, dhidden, 0.0)
-    gb[...] += fold_lanes(dfull)
-    dpre = dfull.astype(BF16)
+    live = hidden > 0
+    gb[...] += fold_lanes(jnp.where(live, dhidden, 0.0))
+    dpre = jnp.where(live, dhidden.astype(BF16), jnp.zeros_like(hidden))
     gw[...] += dot_nt(dpre, jnp.concatenate([ft_ref[step], agg_ref[step]], axis=0))
     dagg = dot_nn(wn_ref[...], dpre)
     dsum_ref[step] = (dagg * inv_ref[step]).astype(BF16)
@@ -365,15 +368,15 @@
     smem = pl.BlockSpec(memory_space=pltpu.SMEM)
     sds = jax.ShapeDtypeStruct
 
-    me = lax.axis_index("dom").reshape(1).astype(I32)
+    link_rows = 2 * links * cap // LANES
     packed, place = pl.pallas_call(
         functools.partial(pack_kernel, n, cap),
         name="pack",
-        out_shape=(sds((n, cap + 2 * links, width), BF16), sds((slots, hub_dev), BF16)),
-        in_specs=[smem, any_space, any_space, any_space],
+        out_shape=(sds((n, cap + link_rows, width), BF16), sds((slots, hub_dev), BF16)),
+        in_specs=[any_space, any_space, any_space],
         out_specs=(any_space, any_space),
         compiler_params=params(),
-    )(me, off_chip(hub_feats), off_chip(hub_mirrors.T), off_chip(hub_links.transpose(1, 2, 0)))
+    )(off_chip(hub_feats), off_chip(hub_mirrors.T), off_chip(hub_links.transpose(1, 2, 0)))
     recv = exchange(packed)
 
     parts = 8
@@ -396,14 +399,14 @@
                 whole(hidden_rows // LANES, LANES),
             ],
             out_specs=[
-                pl.BlockSpec((per_step // parts, span, width), lambda i, *_: (i, 0, 0))
+                pl.BlockSpec((per_step // parts, width, span), lambda i, *_: (i, 0, 0))
             ]
             + [any_space] * 4
             + [whole(hidden_rows, class_rows), any_space],
             scratch_shapes=[pltpu.VMEM((row_blocks, LANES, 2 * width), BF16)],
         ),
         out_shape=(
-            pltpu.HBM((steps, span, width), F32),
+            pltpu.HBM((steps, width, span), F32),
             on_chip((steps, width, span), BF16),
             on_chip((steps, 1, span), F32),
             on_chip((hidden_rows, 2 * width), BF16),
@@ -425,7 +428,7 @@
         functools.partial(forward_kernel, n, cap, links, classes, span),
         name="forward",
         grid=(steps,),
-        in_specs=[any_space, pl.BlockSpec((1, span, width), lambda i: (i, 0, 0))]
+        in_specs=[any_space, pl.BlockSpec((1, width, span), lambda i: (i, 0, 0))]
         + [any_space] * 8,
         out_specs=[any_space] * 3 + [tile_at] + [any_space] * 3,
         out_shape=(
@@ -438,7 +441,7 @@
             sds((n, 1, LANES), F32),
         ),
         scratch_shapes=[
-            pltpu.VMEM((slots, 2 * width), BF16),
+            pltpu.VMEM((width + 16, slots), BF16),
             pltpu.VMEM((links, slots), I32),
             pltpu.VMEM((links, slots), I32),
             pltpu.VMEM((group_total, LANES), F32),

time: 101 us -> 98.3 us (0.973)
  Pallas kernels: 47.6 us -> 45.4 us
  waiting for transfers between devices: 10.8 us -> 9.38 us
    pallas_call x1, Pallas kernels: 18.2 us -> 16.4 us  [on_device(): pl.pallas_call(functools.partial(forward_kernel, n, cap, links, classes,...]
    all_to_all x2, waiting for transfers between devices: 10.8 us -> 9.38 us  [exchange(): return lax.all_to_all(x, 'dom', split_axis=0, concat_axis=0, tiled=True)]
where the time goes in v3:
time: 98.3 us; the launch traced here: 97.7 us
  Pallas kernels  45.4 us (46%)
  blocking collectives  32.3 us (33%)
  starting transfers between devices  9.91 us (10%)
  waiting for transfers between devices  9.38 us (10%)
    all_to_all x2, blocking collectives, exchange(): return lax.all_to_all(x, 'dom', split_axis=0, concat_axis=0, tiled=True)  32.3 us
    pallas_call x1, Pallas kernels, on_device(): pl.pallas_call(functools.partial(forward_kernel, n, cap, links, classes,...  16.4 us
    all_to_all x2, starting transfers between devices, exchange(): return lax.all_to_all(x, 'dom', split_axis=0, concat_axis=0, tiled=True)  9.91 us
    pallas_call x1, Pallas kernels, on_device(): pl.pallas_call(functools.partial(local_kernel, tiles), name='local', grid...  9.57 us
    all_to_all x2, waiting for transfers between devices, exchange(): return lax.all_to_all(x, 'dom', split_axis=0, concat_axis=0, tiled=True)  9.38 us
    pallas_call x1, Pallas kernels, on_device(): pl.pallas_call(functools.partial(backward_kernel, span), name='backward',...  8.9 us
    pallas_call x1, Pallas kernels, on_device(): pl.pallas_call(slot_kernel, name='slots', grid=(steps,), in_specs=[any_sp...  7.36 us
    pallas_call x1, Pallas kernels, on_device(): pl.pallas_call(functools.partial(pack_kernel, n, cap), name='pack', out_s...  2.07 us
  transfers between devices with their start and end apart: 2, of which 2 were waited for; matrix products, arithmetic and copies ran while one was open for 0% of the time, Pallas kernels for 17%

profile of v3, /device:TPU:0, one launch (start us, length us, event | category | flops | bytes accessed | tf_op | source)
XLA Modules:
  0.0 97.7 jit_solution(11950690282780530641)
XLA Ops:
  0.6 2.1 %pack.1 = (bf16[32,36,128]{2,1,0:T(8,128)(2,1)}, bf16[1024,64]{1,0:T(8,128)(2,1)S(1)}) custom-call(bf16[64,128]{1,0:T(8,128)(2,1)} %hub_ref.1, s32[8,64]{1,0:T(8,128)} %bitcast.18, s32[8,8,64]{2,1,0:T(8,128)} %bitcast.17), custom_call_target="tpu_custom_call" | custom-call | tf_op jit(solution)/shard_map/pack/pallas_call | solution.py:372
  2.7 7.3 %all-to-all-start = ((bf16[32,36,128]{2,1,0:T(8,128)(2,1)}), bf16[32,36,128]{2,1,0:T(8,128)(2,1)S(1)}, u32[]{:S(2)}, u32[]{:S(2)}) async-start(bf16[32,36,128]{2,1,0:T(8,128)(2,1)} %get-tuple-element.32), calls=%async_computation | async-start | bytes 655360 | tf_op jit(solution)/shard_map/all_to_all | solution.py:349
  10.0 0.0 copy-start.2
  10.0 0.0 copy-start.3
  10.0 0.0 copy-start.4
  10.0 9.6 %local.1 = (f32[6,128,1024]{2,1,0:T(8,128)}, bf16[6,128,1024]{2,1,0:T(8,128)(2,1)S(1)}, f32[6,1,1024]{2,1,0:T(1,128)S(1)}, bf16[512,256]{1,0:T(8,128)(2,1)S(1)},...) custom-call(s32[4,48]{1,0:T(4,128)} %bitcast.19, bf16[6144,128]{1,0:T(8,128)(2,1)} %feats_ref.1, ...), custom_call_target="tpu_custom_call" | custom-call | tf_op jit(solution)/shard_map/local/pallas_call | solution.py:387
  19.6 0.0 copy-start
  19.6 0.0 copy-start.5
  19.6 2.4 %all-to-all-done.recv_ref = bf16[32,36,128]{2,1,0:T(8,128)(2,1)S(1)} async-done(((bf16[32,36,128]{2,1,0:T(8,128)(2,1)}), bf16[32,36,128]{2,1,0:T(8,128)(2,1)S(1)}, u32[]{:S(2)}, u32[]{:S(2)}) %all-to-all-start) | async-done | bytes 294944 | tf_op jit(solution)/shard_map/all_to_all | solution.py:349
  22.0 0.0 copy-start.1
  22.0 0.0 copy-done.2
  22.0 0.0 copy-done.3
  22.0 0.0 copy-done.4
  22.0 16.4 %forward.1 = (bf16[6,128,1024]{2,1,0:T(8,128)(2,1)S(1)}, bf16[6,512,1024]{2,1,0:T(8,128)(2,1)S(1)}, f32[6,176,1024]{2,1,0:T(8,128)S(1)}, bf16[6,1024,1024]{2,1,0...) custom-call(bf16[32,36,128]{2,1,0:T(8,128)(2,1)S(1)} %all-to-all-done.recv_ref, ...), custom_call_target="tpu_custom_call" | custom-call | tf_op jit(solution)/shard_map/forward/pallas_call | solution.py:427
  38.4 10.5 %all_to_all.20.sums_ref = f32[32,1,128]{2,1,0:T(1,128)S(1)} all-to-all(f32[32,1,128]{2,1,0:T(1,128)S(1)} %get-tuple-element.39), channel_id=1, replica_groups=mesh['dom'=32] {'dom'}, dimensions={0} | all-to-all | bytes 32768 | tf_op jit(solution)/shard_map/all_to_all | solution.py:349
  48.9 0.0 copy-done
  48.9 0.0 copy-done.5
  48.9 0.0 copy-done.1
  48.9 8.9 %backward.1 = (bf16[32,56,128]{2,1,0:T(8,128)(2,1)}, f32[1,1]{1,0:T(1,128)}, bf16[6,128,1024]{2,1,0:T(8,128)(2,1)S(1)}) custom-call(f32[32,1,128]{2,1,0:T(1,128)S(1)} %all_to_all.20.sums_ref, f32[1,64]{1,0:T(1,128)S(1)} %bitcast.15, f32[6,176,1024]{2,1,0:T(8,128)S(1)} %get-tuple-element.40.pmo_ref, bf16[6,512,1024]{2,1,0:T(8,128)(2,1)S(1)} %get-tuple-element.41.hid_ref, ...), custom_call_target="tpu_custom_call" | custom-call | tf_op jit(solution)/shard_map/backward/pallas_call | solution.py:459
  57.8 2.6 %all-to-all-start.2 = ((bf16[32,56,128]{2,1,0:T(8,128)(2,1)}), bf16[32,56,128]{2,1,0:T(8,128)(2,1)S(1)}, u32[]{:S(2)}, u32[]{:S(2)}) async-start(bf16[32,56,128]{2,1,0:T(8,128)(2,1)} %get-tuple-element.47), calls=%async_computation.2 | async-start | bytes 917504 | tf_op jit(solution)/shard_map/all_to_all | solution.py:349
  60.4 7.4 %slots.1 = (bf16[32,32,128]{2,1,0:T(8,128)(2,1)S(1)}, bf16[64,1024]{1,0:T(8,128)(2,1)S(1)}) custom-call(bf16[6,128,1024]{2,1,0:T(8,128)(2,1)S(1)} %get-tuple-element.48.dsum_ref, bf16[6,1024,1024]{2,1,0:T(8,128)(2,1)} %get-tuple-element.49.m_ref, bf16[1024,64]{1,0:T(8,128)(2,1)S(1)} %get-tuple-element.50.place_ref), custom_call_target="tpu_custom_call" | custom-call | tf_op jit(solution)/shard_map/slots/pallas_call | solution.py:482
  67.8 7.0 %all-to-all-done.2.recv_ref = bf16[32,56,128]{2,1,0:T(8,128)(2,1)S(1)} async-done(((bf16[32,56,128]{2,1,0:T(8,128)(2,1)}), bf16[32,56,128]{2,1,0:T(8,128)(2,1)S(1)}, u32[]{:S(2)}, u32[]{:S(2)}) %all-to-all-start.2) | async-done | bytes 458784 | tf_op jit(solution)/shard_map/all_to_all | solution.py:349
  74.8 0.1 reduce.1
  74.9 21.8 %all_to_all.21.recv_ref = bf16[32,88,128]{2,1,0:T(8,128)(2,1)S(1)} all-to-all(bf16[32,88,128]{2,1,0:T(8,128)(2,1)S(1)} %reduce.1), channel_id=1, replica_groups=mesh['dom'=32] {'dom'}, dimensions={0} | all-to-all | bytes 1441792 | tf_op jit(solution)/shard_map/all_to_all | solution.py:349
  96.7 1.1 %final.1 = (f32[128,512]{1,0:T(8,128)}, f32[128,512]{1,0:T(8,128)}, f32[4,128]{1,0:T(4,128)}, f32[172,512]{1,0:T(8,128)}, f32[64,128]{1,0:T(8,128)}) custom-call(bf16[32,88,128]{2,1,0:T(8,128)(2,1)S(1)} %all_to_all.21.recv_ref, bf16[64,1024]{1,0:T(8,128)(2,1)S(1)} %get-tuple-element.52.place_ref), custom_call_target="tpu_custom_call" | custom-call | tf_op jit(solution)/shard_map/final/pallas_call | solution.py:501
Async XLA Ops:
  2.7 19.3 %all-to-all-start = ((bf16[32,36,128]{2,1,0:T(8,128)(2,1)}), bf16[32,36,128]{2,1,0:T(8,128)(2,1)S(1)}, u32[]{:S(2)}, u32[]{:S(2)}) async-start(bf16[32,36,128]{2,1,0:T(8,128)(2,1)} %get-tuple-element.32), calls=%async_computation | async-start | bytes 655360 | tf_op jit(solution)/shard_map/all_to_all | solution.py:349
  10.0 12.0 %copy-start.2 = (s32[6144]{0:T(1024)S(1)}, s32[6144]{0:T(1024)}, u32[]{:S(2)}) copy-start(s32[6144]{0:T(1024)} %param.20) | copy-start | bytes 73732
  10.0 12.0 %copy-start.3 = (s32[6144]{0:T(1024)S(1)}, s32[6144]{0:T(1024)}, u32[]{:S(2)}) copy-start(s32[6144]{0:T(1024)} %param.21) | copy-start | bytes 73732
  10.0 12.0 %copy-start.4 = (s32[6144]{0:T(1024)S(1)}, s32[6144]{0:T(1024)}, u32[]{:S(2)}) copy-start(s32[6144]{0:T(1024)} %param.22) | copy-start | bytes 73732
  19.6 29.3 %copy-start = (bf16[128,512]{1,0:T(8,128)(2,1)S(1)}, bf16[128,512]{1,0:T(8,128)(2,1)}, u32[]{:S(2)}) copy-start(bf16[128,512]{1,0:T(8,128)(2,1)} %wn_ref.3) | copy-start | bytes 393220
  19.6 29.3 %copy-start.5 = (f32[64]{0:T(128)S(1)}, f32[64]{0:T(128)}, u32[]{:S(2)}) copy-start(f32[64]{0:T(128)} %param.27) | copy-start | bytes 772
  22.0 26.9 %copy-start.1 = (bf16[512,176]{1,0:T(8,128)(2,1)S(1)}, bf16[512,176]{1,0:T(8,128)(2,1)}, u32[]{:S(2)}) copy-start(bf16[512,176]{1,0:T(8,128)(2,1)} %get-tuple-element.45.wc_ref) | copy-start | bytes 540676
  57.8 17.0 %all-to-all-start.2 = ((bf16[32,56,128]{2,1,0:T(8,128)(2,1)}), bf16[32,56,128]{2,1,0:T(8,128)(2,1)S(1)}, u32[]{:S(2)}, u32[]{:S(2)}) async-start(bf16[32,56,128]{2,1,0:T(8,128)(2,1)} %get-tuple-element.47), calls=%async_computation.2 | async-start | bytes 917504 | tf_op jit(solution)/shard_map/all_to_all | solution.py:349

commit v4 on v3

--- a/solution.py
+++ b/solution.py
@@ -46,7 +46,7 @@
     return pltpu.CompilerParams(vmem_limit_bytes=mib << 20, **kw)
 
 
-def pack_kernel(n, cap, hub_ref, mir_ref, link_ref, out_ref, place_ref):
+def pack_kernel(n, cap, _, hub_ref, mir_ref, link_ref, out_ref, place_ref):
     hubs, width = hub_ref.shape
     mirrors, links = link_ref.shape[0], link_ref.shape[1]
     dest = iota((n, hubs), 0)
@@ -215,7 +215,7 @@
     hot = class_row == lane_row(label_ref, step, parts)
     picked = jnp.sum(jnp.where(hot, logits, 0.0), axis=0, keepdims=True)
     loss = (top + jnp.log(total) - picked) * mask
-    pmo_ref[step] = mask * (shifted * (1.0 / total) - jnp.where(hot, 1.0, 0.0))
+    pmo_ref[step] = shifted * (mask / total) - jnp.where(hot, mask, 0.0)
     group_row = lane_row(group_ref, step, parts)
     of_ref[step] = group_row
     in_group = iota((groups, span), 0) == group_row
@@ -236,12 +236,12 @@
 
 def backward_kernel(
     span,
-    sums_ref, logw_ref, pmo_ref, hid_ref, ft_ref, agg_ref, inv_ref, group_ref, wc_ref, wn_ref,
-    msg_ref, obj_ref, dsum_ref,
+    me_ref, sums_ref, logw_ref, pmo_ref, hid_ref, ft_ref, agg_ref, inv_ref, group_ref, wc_ref, wn_ref,
+    own_ref, pass_ref, obj_ref, dsum_ref,
     q_col, gw, gwc, gb, flat,
 ):
     step = pl.program_id(0)
-    n, share = msg_ref.shape[0], msg_ref.shape[1]
+    half, share = pass_ref.shape[0], pass_ref.shape[1]
     groups = logw_ref.shape[1]
     hidden_rows = gb.shape[0]
     class_rows = pmo_ref.shape[1]
@@ -289,8 +289,12 @@
         for b in range(hidden_rows // LANES):
             col = jnp.sum(gb[b * LANES : (b + 1) * LANES, :], axis=1, keepdims=True)
             flat[row + b : row + b + 1, :] = to_row(jnp.broadcast_to(col, (LANES, LANES)))
-        for d in range(n):
-            msg_ref[d] = flat[d * share : (d + 1) * share, :].astype(BF16)
+        core = me_ref[0] % 2
+        for d in range(half):
+            own_at = pl.multiple_of((2 * d + core) * share, 8)
+            own_ref[d] = flat[pl.ds(own_at, share), :]
+            pass_at = pl.multiple_of((2 * d + 1 - core) * share, 8)
+            pass_ref[d] = flat[pl.ds(pass_at, share), :].astype(BF16)
 
 
 def slot_kernel(dsum_ref, m_ref, place_ref, out_ref, turned_ref, slot):
@@ -305,7 +309,11 @@
             at = slice(b * LANES, (b + 1) * LANES)
             turned_ref[:, at] = turn(place_ref[at, :]).astype(BF16)
 
-    slot[...] += dot_nn(dsum_ref[step], m_ref[0])
+    total = slot[...]
+    blocks = m_ref.shape[0]
+    for k in range(blocks):
+        total = total + dot_nn(dsum_ref[step * blocks + k], m_ref[k])
+    slot[...] = total
 
     @pl.when(step == pl.num_programs(0) - 1)
     def _():
@@ -315,11 +323,15 @@
             out_ref[b * per : (b + 1) * per] = rows.reshape(per, cap, LANES).astype(BF16)
 
 
+def pair_kernel(own_ref, recv_ref, out_ref):
+    out_ref[...] = (own_ref[...] + recv_ref[...].astype(F32)).astype(BF16)
+
+
 def reduce_kernel(recv_ref, slot_ref, out_ref):
     n, cap, width = slot_ref.shape
     share = recv_ref.shape[1]
     total = recv_ref[0].astype(F32)
-    for d in range(1, n):
+    for d in range(1, recv_ref.shape[0]):
         total = total + recv_ref[d].astype(F32)
     total = total.astype(BF16)
     out_ref[:, 0:cap, :] = slot_ref[...]
@@ -369,14 +381,15 @@
     sds = jax.ShapeDtypeStruct
 
     link_rows = 2 * links * cap // LANES
+    me = lax.axis_index("dom").reshape(1).astype(I32)
     packed, place = pl.pallas_call(
         functools.partial(pack_kernel, n, cap),
         name="pack",
         out_shape=(sds((n, cap + link_rows, width), BF16), sds((slots, hub_dev), BF16)),
-        in_specs=[any_space, any_space, any_space],
+        in_specs=[smem, any_space, any_space, any_space],
         out_specs=(any_space, any_space),
         compiler_params=params(),
-    )(off_chip(hub_feats), off_chip(hub_mirrors.T), off_chip(hub_links.transpose(1, 2, 0)))
+    )(me, off_chip(hub_feats), off_chip(hub_mirrors.T), off_chip(hub_links.transpose(1, 2, 0)))
     recv = exchange(packed)
 
     parts = 8
@@ -456,14 +469,16 @@
 
     grad_rows = hidden_rows // LANES * (2 * width + class_rows + 1)
     share = -(-grad_rows // (8 * n)) * 8
-    message, objective, dsum = pl.pallas_call(
+    half = n // 2
+    own, passed, objective, dsum = pl.pallas_call(
         functools.partial(backward_kernel, span),
         name="backward",
         grid=(steps,),
-        in_specs=[any_space] * 10,
-        out_specs=[any_space, smem, any_space],
+        in_specs=[smem] + [any_space] * 10,
+        out_specs=[any_space, any_space, smem, any_space],
         out_shape=(
-            pltpu.HBM((n, share, LANES), BF16), sds((1, 1), F32), on_chip((steps, width, span), BF16),
+            on_chip((half, share, LANES), F32), pltpu.HBM((half, share, LANES), BF16),
+            sds((1, 1), F32), on_chip((steps, width, span), BF16),
         ),
         scratch_shapes=[
             pltpu.VMEM((group_total, LANES), F32),
@@ -474,20 +489,33 @@
         ],
         compiler_params=params(1),
     )(
-        all_sums, group_logw.reshape(1, group_total), keep(pmo), keep(hid), keep(f_turned),
+        me, all_sums, group_logw.reshape(1, group_total), keep(pmo), keep(hid), keep(f_turned),
         keep(agg), keep(inv), keep(group_rows), keep(wc_rows), keep(w_neigh),
     )
-    answer = exchange(message)
-
+    other = lax.ppermute(passed, "dom", [(i, i ^ 1) for i in range(n)])
+    paired = pl.pallas_call(
+        pair_kernel,
+        name="pair",
+        out_shape=pltpu.HBM((half, share, LANES), BF16),
+        in_specs=[any_space, any_space],
+        out_specs=any_space,
+        compiler_params=params(),
+    )(keep(own), keep(other))
+    same_core = [list(range(core, n, 2)) for core in range(2)]
+    answer = lax.all_to_all(
+        paired, "dom", split_axis=0, concat_axis=0, tiled=True, axis_index_groups=same_core
+    )
+
+    blocks = 2 if steps % 2 == 0 else 1
     slot_grads, place_turned = pl.pallas_call(
         slot_kernel,
         name="slots",
-        grid=(steps,),
-        in_specs=[any_space, tile_at, any_space],
+        grid=(steps // blocks,),
+        in_specs=[any_space, pl.BlockSpec((blocks, span, slots), lambda i: (i, 0, 0)), any_space],
         out_specs=[any_space] * 2,
         out_shape=(on_chip((n, cap, width), BF16), on_chip((hub_dev, slots), BF16)),
         scratch_shapes=[pltpu.VMEM((width, slots), F32)],
-        compiler_params=params(1),
+        compiler_params=params(1, 20),
     )(keep(dsum), off_chip(counts), keep(place))
     reduced = pl.pallas_call(
         reduce_kernel,

time: 98.3 us -> 96.8 us (0.985)
  waiting for transfers between devices: 9.38 us -> 7.59 us
  starting transfers between devices: 9.91 us -> 10.9 us
    all_to_all x2 -> x1, waiting for transfers between devices: 9.38 us -> 2.36 us  [exchange(): return lax.all_to_all(x, 'dom', split_axis=0, concat_axis=0, tiled=True)]
    all_to_all x0 -> x1, waiting for transfers between devices: none -> 3.55 us  [on_device(): lax.all_to_all(paired, 'dom', split_axis=0, concat_axis=0, tiled=True, ax...]
    all_to_all x0 -> x1, starting transfers between devices: none -> 3.53 us  [on_device(): lax.all_to_all(paired, 'dom', split_axis=0, concat_axis=0, tiled=True, ax...]
    all_to_all x2 -> x1, starting transfers between devices: 9.91 us -> 7.3 us  [exchange(): return lax.all_to_all(x, 'dom', split_axis=0, concat_axis=0, tiled=True)]
    ppermute x0 -> x1, waiting for transfers between devices: none -> 1.69 us  [on_device(): other = lax.ppermute(passed, 'dom', [(i, i ^ 1) for i in range(n)])]
    pallas_call x1 -> x2, Pallas kernels: 7.36 us -> 6.95 us  [the longest x1 6.23 us: on_device(): pl.pallas_call(slot_kernel, name='slots', grid=(steps // blocks,), in_spe...]
  transfers between devices with their start and end apart: 2 -> 3, of which waited for: 2 -> 3; matrix products, arithmetic and copies ran while one was open for 0% -> 0% of each run, Pallas kernels for 17% -> 16%
where the time goes in v4:
time: 96.8 us; the launch traced here: 96.2 us
  Pallas kernels  45 us (46%)
  blocking collectives  31.9 us (33%)
  starting transfers between devices  10.9 us (11%)
  waiting for transfers between devices  7.59 us (8%)
    all_to_all x2, blocking collectives, exchange(): return lax.all_to_all(x, 'dom', split_axis=0, concat_axis=0, tiled=True)  31.9 us
    pallas_call x1, Pallas kernels, on_device(): pl.pallas_call(functools.partial(forward_kernel, n, cap, links, classes,...  16.4 us
    pallas_call x1, Pallas kernels, on_device(): pl.pallas_call(functools.partial(local_kernel, tiles), name='local', grid...  9.59 us
    pallas_call x1, Pallas kernels, on_device(): pl.pallas_call(functools.partial(backward_kernel, span), name='backward',...  8.88 us
    all_to_all x1, starting transfers between devices, exchange(): return lax.all_to_all(x, 'dom', split_axis=0, concat_axis=0, tiled=True)  7.3 us
    pallas_call x1, Pallas kernels, on_device(): pl.pallas_call(slot_kernel, name='slots', grid=(steps // blocks,), in_spe...  6.23 us
    all_to_all x1, waiting for transfers between devices, on_device(): lax.all_to_all(paired, 'dom', split_axis=0, concat_axis=0, tiled=True, ax...  3.55 us
    all_to_all x1, starting transfers between devices, on_device(): lax.all_to_all(paired, 'dom', split_axis=0, concat_axis=0, tiled=True, ax...  3.53 us
  transfers between devices with their start and end apart: 3, of which 3 were waited for; matrix products, arithmetic and copies ran while one was open for 0% of the time, Pallas kernels for 16%

profile of v4, /device:TPU:0, one launch (start us, length us, event | category | flops | bytes accessed | tf_op | source)
XLA Modules:
  0.0 96.2 jit_solution(1484342447675975239)
XLA Ops:
  0.6 2.1 %pack.1 = (bf16[32,36,128]{2,1,0:T(8,128)(2,1)}, bf16[1024,64]{1,0:T(8,128)(2,1)S(1)}) custom-call(s32[1]{0:T(128)} %bitcast._.me_ref, bf16[64,128]{1,0:T(8,128)(2,1)} %hub_ref.1, s32[8,64]{1,0:T(8,128)} %bitcast.19, s32[8,8,64]{2,1,0:T(8,128)} %bitcast.18), custom_call_target="tpu_custom_call" | custom-call | tf_op jit(solution)/shard_map/pack/pallas_call | solution.py:385
  2.7 7.3 %all-to-all-start = ((bf16[32,36,128]{2,1,0:T(8,128)(2,1)}), bf16[32,36,128]{2,1,0:T(8,128)(2,1)S(1)}, u32[]{:S(2)}, u32[]{:S(2)}) async-start(bf16[32,36,128]{2,1,0:T(8,128)(2,1)} %get-tuple-element.33), calls=%async_computation | async-start | bytes 655360 | tf_op jit(solution)/shard_map/all_to_all | solution.py:361
  10.0 0.0 copy-start.2
  10.0 0.0 copy-start.3
  10.0 0.0 copy-start.4
  10.0 9.6 %local.1 = (f32[6,128,1024]{2,1,0:T(8,128)}, bf16[6,128,1024]{2,1,0:T(8,128)(2,1)S(1)}, f32[6,1,1024]{2,1,0:T(1,128)S(1)}, bf16[512,256]{1,0:T(8,128)(2,1)S(1)},...) custom-call(s32[4,48]{1,0:T(4,128)} %bitcast.20, bf16[6144,128]{1,0:T(8,128)(2,1)} %feats_ref.1, ...), custom_call_target="tpu_custom_call" | custom-call | tf_op jit(solution)/shard_map/local/pallas_call | solution.py:400
  19.6 0.0 copy-start
  19.6 0.0 copy-start.5
  19.6 2.4 %all-to-all-done.recv_ref = bf16[32,36,128]{2,1,0:T(8,128)(2,1)S(1)} async-done(((bf16[32,36,128]{2,1,0:T(8,128)(2,1)}), bf16[32,36,128]{2,1,0:T(8,128)(2,1)S(1)}, u32[]{:S(2)}, u32[]{:S(2)}) %all-to-all-start) | async-done | bytes 294944 | tf_op jit(solution)/shard_map/all_to_all | solution.py:361
  22.0 0.0 copy-start.1
  22.0 0.0 copy-done.2
  22.0 0.0 copy-done.3
  22.0 0.0 copy-done.4
  22.0 16.4 %forward.1 = (bf16[6,128,1024]{2,1,0:T(8,128)(2,1)S(1)}, bf16[6,512,1024]{2,1,0:T(8,128)(2,1)S(1)}, f32[6,176,1024]{2,1,0:T(8,128)S(1)}, bf16[6,1024,1024]{2,1,0...) custom-call(bf16[32,36,128]{2,1,0:T(8,128)(2,1)S(1)} %all-to-all-done.recv_ref, ...), custom_call_target="tpu_custom_call" | custom-call | tf_op jit(solution)/shard_map/forward/pallas_call | solution.py:440
  38.4 10.5 %all_to_all.20.sums_ref = f32[32,1,128]{2,1,0:T(1,128)S(1)} all-to-all(f32[32,1,128]{2,1,0:T(1,128)S(1)} %get-tuple-element.40), channel_id=1, replica_groups=mesh['dom'=32] {'dom'}, dimensions={0} | all-to-all | bytes 32768 | tf_op jit(solution)/shard_map/all_to_all | solution.py:361
  48.9 0.0 copy-done
  48.9 0.0 copy-done.5
  48.9 0.0 copy-done.1
  48.9 8.9 %backward.1 = (f32[16,56,128]{2,1,0:T(8,128)S(1)}, bf16[16,56,128]{2,1,0:T(8,128)(2,1)}, f32[1,1]{1,0:T(1,128)}, bf16[6,128,1024]{2,1,0:T(8,128)(2,1)S(1)}) custom-call(s32[1]{0:T(128)} %bitcast._.me_ref, f32[32,1,128]{2,1,0:T(1,128)S(1)} %all_to_all.20.sums_ref, f32[1,64]{1,0:T(1,128)S(1)} %bitcast.16, f32[6,176,1024]{2,1,0:T(8,128)S(1)} %get-tuple-element.41.pmo_ref, ...), custom_call_target="tpu_custom_call" | custom-call | tf_op jit(solution)/shard_map/backward/pallas_call | solution.py:473
  57.8 0.1 collective-permute-start
  57.9 1.7 %collective-permute-done.recv_ref = bf16[16,56,128]{2,1,0:T(8,128)(2,1)S(1)} collective-permute-done((bf16[16,56,128]{2,1,0:T(8,128)(2,1)}, bf16[16,56,128]{2,1,0:T(8,128)(2,1)S(1)}, u32[]{:S(2)}, u32[]{:S(2)}) %collective-permute-start) | collective-permute-done | bytes 229408 | tf_op jit(solution)/shard_map/ppermute | solution.py:495
  59.6 0.7 pair.1
  60.3 3.5 %all-to-all-start.2 = ((bf16[16,56,128]{2,1,0:T(8,128)(2,1)}), bf16[16,56,128]{2,1,0:T(8,128)(2,1)S(1)}, u32[]{:S(2)}, u32[]{:S(2)}) async-start(bf16[16,56,128]{2,1,0:T(8,128)(2,1)} %pair.1), calls=%async_computation.2 | async-start | bytes 458752 | tf_op jit(solution)/shard_map/all_to_all | solution.py:505
  63.8 6.2 %slots.1 = (bf16[32,32,128]{2,1,0:T(8,128)(2,1)S(1)}, bf16[64,1024]{1,0:T(8,128)(2,1)S(1)}) custom-call(bf16[6,128,1024]{2,1,0:T(8,128)(2,1)S(1)} %get-tuple-element.50.dsum_ref, bf16[6,1024,1024]{2,1,0:T(8,128)(2,1)} %get-tuple-element.51.m_ref, bf16[1024,64]{1,0:T(8,128)(2,1)S(1)} %get-tuple-element.52.place_ref), custom_call_target="tpu_custom_call" | custom-call | tf_op jit(solution)/shard_map/slots/pallas_call | solution.py:510
  70.1 3.5 %all-to-all-done.2.recv_ref = bf16[16,56,128]{2,1,0:T(8,128)(2,1)S(1)} async-done(((bf16[16,56,128]{2,1,0:T(8,128)(2,1)}), bf16[16,56,128]{2,1,0:T(8,128)(2,1)S(1)}, u32[]{:S(2)}, u32[]{:S(2)}) %all-to-all-start.2) | async-done | bytes 229408 | tf_op jit(solution)/shard_map/all_to_all | solution.py:505
  73.6 0.1 reduce.1
  73.7 21.4 %all_to_all.21.recv_ref = bf16[32,88,128]{2,1,0:T(8,128)(2,1)S(1)} all-to-all(bf16[32,88,128]{2,1,0:T(8,128)(2,1)S(1)} %reduce.1), channel_id=1, replica_groups=mesh['dom'=32] {'dom'}, dimensions={0} | all-to-all | bytes 1441792 | tf_op jit(solution)/shard_map/all_to_all | solution.py:361
  95.1 1.1 %final.1 = (f32[128,512]{1,0:T(8,128)}, f32[128,512]{1,0:T(8,128)}, f32[4,128]{1,0:T(4,128)}, f32[172,512]{1,0:T(8,128)}, f32[64,128]{1,0:T(8,128)}) custom-call(bf16[32,88,128]{2,1,0:T(8,128)(2,1)S(1)} %all_to_all.21.recv_ref, bf16[64,1024]{1,0:T(8,128)(2,1)S(1)} %get-tuple-element.54.place_ref), custom_call_target="tpu_custom_call" | custom-call | tf_op jit(solution)/shard_map/final/pallas_call | solution.py:529
Async XLA Ops:
  2.7 19.3 %all-to-all-start = ((bf16[32,36,128]{2,1,0:T(8,128)(2,1)}), bf16[32,36,128]{2,1,0:T(8,128)(2,1)S(1)}, u32[]{:S(2)}, u32[]{:S(2)}) async-start(bf16[32,36,128]{2,1,0:T(8,128)(2,1)} %get-tuple-element.33), calls=%async_computation | async-start | bytes 655360 | tf_op jit(solution)/shard_map/all_to_all | solution.py:361
  10.0 12.0 %copy-start.2 = (s32[6144]{0:T(1024)S(1)}, s32[6144]{0:T(1024)}, u32[]{:S(2)}) copy-start(s32[6144]{0:T(1024)} %param.20) | copy-start | bytes 73732
  10.0 12.0 %copy-start.3 = (s32[6144]{0:T(1024)S(1)}, s32[6144]{0:T(1024)}, u32[]{:S(2)}) copy-start(s32[6144]{0:T(1024)} %param.21) | copy-start | bytes 73732
  10.0 12.0 %copy-start.4 = (s32[6144]{0:T(1024)S(1)}, s32[6144]{0:T(1024)}, u32[]{:S(2)}) copy-start(s32[6144]{0:T(1024)} %param.22) | copy-start | bytes 73732
  19.6 29.3 %copy-start = (bf16[128,512]{1,0:T(8,128)(2,1)S(1)}, bf16[128,512]{1,0:T(8,128)(2,1)}, u32[]{:S(2)}) copy-start(bf16[128,512]{1,0:T(8,128)(2,1)} %wn_ref.3) | copy-start | bytes 393220
  19.6 29.3 %copy-start.5 = (f32[64]{0:T(128)S(1)}, f32[64]{0:T(128)}, u32[]{:S(2)}) copy-start(f32[64]{0:T(128)} %param.27) | copy-start | bytes 772
  22.0 26.9 %copy-start.1 = (bf16[512,176]{1,0:T(8,128)(2,1)S(1)}, bf16[512,176]{1,0:T(8,128)(2,1)}, u32[]{:S(2)}) copy-start(bf16[512,176]{1,0:T(8,128)(2,1)} %get-tuple-element.46.wc_ref) | copy-start | bytes 540676
  57.8 1.8 %collective-permute-start = (bf16[16,56,128]{2,1,0:T(8,128)(2,1)}, bf16[16,56,128]{2,1,0:T(8,128)(2,1)S(1)}, u32[]{:S(2)}, u32[]{:S(2)}) collective-permute-start(bf16[16,56,128]{2,1,0:T(8,128)(2,1)} %get-tuple-element.49), channel_id=1, source_target_pairs={{0,1},{1,0},{2,3},{3,2},{4,5},{5,4},{6,7},{7,6},{8,9},{9,8},{10,11... | collective-permute-start | bytes 688136 | tf_op jit(solution)/shard_map/ppermute | solution.py:495
  60.3 13.3 %all-to-all-start.2 = ((bf16[16,56,128]{2,1,0:T(8,128)(2,1)}), bf16[16,56,128]{2,1,0:T(8,128)(2,1)S(1)}, u32[]{:S(2)}, u32[]{:S(2)}) async-start(bf16[16,56,128]{2,1,0:T(8,128)(2,1)} %pair.1), calls=%async_computation.2 | async-start | bytes 458752 | tf_op jit(solution)/shard_map/all_to_all | solution.py:505

commit v5 on v4

--- a/solution.py
+++ b/solution.py
@@ -328,22 +328,29 @@
 
 
 def reduce_kernel(recv_ref, slot_ref, out_ref):
-    n, cap, width = slot_ref.shape
-    share = recv_ref.shape[1]
+    n, cap = slot_ref.shape[0], slot_ref.shape[1]
+    part = out_ref.shape[1] - cap
     total = recv_ref[0].astype(F32)
     for d in range(1, recv_ref.shape[0]):
         total = total + recv_ref[d].astype(F32)
-    total = total.astype(BF16)
+    halves = [total[0:part].astype(BF16), total[part:].astype(BF16)]
     out_ref[:, 0:cap, :] = slot_ref[...]
-    out_ref[:, cap:, :] = jnp.broadcast_to(total[None], (n, share, width))
-
-
-def final_kernel(cap, recv_ref, place_ref, gws_ref, gwn_ref, gb_ref, gwc_ref, hub_ref, flat):
-    n, share, width = recv_ref.shape[0], recv_ref.shape[1] - cap, recv_ref.shape[2]
+    for d in range(n):
+        out_ref[d, cap:, :] = halves[d % 2]
+
+
+def final_kernel(
+    cap, me_ref, recv_ref, other_ref, place_ref, gws_ref, gwn_ref, gb_ref, gwc_ref, hub_ref, flat
+):
+    n, part, width = recv_ref.shape[0], recv_ref.shape[1] - cap, recv_ref.shape[2]
     rows = recv_ref[:, 0:cap, :].astype(F32).reshape(n * cap, width).astype(BF16)
     hub_ref[...] = dot_nn(place_ref[...], rows)
+    even = me_ref[0] % 2 == 0
     for d in range(n):
-        flat[d * share : (d + 1) * share, :] = recv_ref[d, cap:, :].astype(F32)
+        mine = recv_ref[d, cap:, :].astype(F32)
+        other = other_ref[d, cap:, :].astype(F32)
+        flat[2 * d * part : (2 * d + 1) * part, :] = jnp.where(even, mine, other)
+        flat[(2 * d + 1) * part : (2 * d + 2) * part, :] = jnp.where(even, other, mine)
     hidden_rows = gws_ref.shape[1]
     classes = gwc_ref.shape[0]
     class_rows = -(-classes // 16) * 16
@@ -520,12 +527,13 @@
     reduced = pl.pallas_call(
         reduce_kernel,
         name="reduce",
-        out_shape=sds((n, cap + share, LANES), BF16),
+        out_shape=sds((n, cap + share // 2, LANES), BF16),
         in_specs=[any_space, any_space],
         out_specs=any_space,
         compiler_params=params(),
     )(keep(answer), keep(slot_grads))
     gathered = exchange(reduced)
+    other_half = lax.ppermute(gathered, "dom", [(i, i ^ 1) for i in range(n)])
     grad_w_self, grad_w_neigh, grad_bias, grad_w_cls, hub_grad = pl.pallas_call(
         functools.partial(final_kernel, cap),
         name="final",
@@ -536,11 +544,11 @@
             sds((classes, hidden_rows), F32),
             sds((hub_dev, width), F32),
         ),
-        in_specs=[any_space, any_space],
+        in_specs=[smem, any_space, any_space, any_space],
         out_specs=(any_space,) * 5,
         scratch_shapes=[pltpu.VMEM((n * share, LANES), F32)],
         compiler_params=params(),
-    )(keep(gathered), keep(place_turned))
+    )(me, keep(gathered), keep(other_half), keep(place_turned))
     return (
         objective.reshape(()), grad_w_self, grad_w_neigh, grad_bias.reshape(hidden_rows),
         grad_w_cls.T, hub_grad,

time: 96.8 us -> 95.1 us (0.982)
  blocking collectives: 31.9 us -> 28.3 us
  waiting for transfers between devices: 7.59 us -> 9.5 us
    all_to_all x2, blocking collectives: 31.9 us -> 28.3 us  [exchange(): return lax.all_to_all(x, 'dom', split_axis=0, concat_axis=0, tiled=True)]
    ppermute x0 -> x1, waiting for transfers between devices: none -> 1.91 us  [on_device(): other_half = lax.ppermute(gathered, 'dom', [(i, i ^ 1) for i in range(n)])]
  transfers between devices with their start and end apart: 3 -> 4, of which waited for: 3 -> 4; matrix products, arithmetic and copies ran while one was open for 0% -> 0% of each run, Pallas kernels for 16% -> 17%
where the time goes in v5:
time: 95.1 us; the launch traced here: 94.5 us
  Pallas kernels  45.1 us (47%)
  blocking collectives  28.3 us (30%)
  starting transfers between devices  10.9 us (11%)
  waiting for transfers between devices  9.5 us (10%)
    all_to_all x2, blocking collectives, exchange(): return lax.all_to_all(x, 'dom', split_axis=0, concat_axis=0, tiled=True)  28.3 us
    pallas_call x1, Pallas kernels, on_device(): pl.pallas_call(functools.partial(forward_kernel, n, cap, links, classes,...  16.4 us
    pallas_call x1, Pallas kernels, on_device(): pl.pallas_call(functools.partial(local_kernel, tiles), name='local', grid...  9.59 us
    pallas_call x1, Pallas kernels, on_device(): pl.pallas_call(functools.partial(backward_kernel, span), name='backward',...  8.87 us
    all_to_all x1, starting transfers between devices, exchange(): return lax.all_to_all(x, 'dom', split_axis=0, concat_axis=0, tiled=True)  7.3 us
    pallas_call x1, Pallas kernels, on_device(): pl.pallas_call(slot_kernel, name='slots', grid=(steps // blocks,), in_spe...  6.23 us
    all_to_all x1, waiting for transfers between devices, on_device(): lax.all_to_all(paired, 'dom', split_axis=0, concat_axis=0, tiled=True, ax...  3.55 us
    all_to_all x1, starting transfers between devices, on_device(): lax.all_to_all(paired, 'dom', split_axis=0, concat_axis=0, tiled=True, ax...  3.53 us
  transfers between devices with their start and end apart: 4, of which 4 were waited for; matrix products, arithmetic and copies ran while one was open for 0% of the time, Pallas kernels for 17%

profile of v5, /device:TPU:0, one launch (start us, length us, event | category | flops | bytes accessed | tf_op | source)
XLA Modules:
  0.0 94.5 jit_solution(9612166194263683152)
XLA Ops:
  0.6 2.1 %pack.1 = (bf16[32,36,128]{2,1,0:T(8,128)(2,1)}, bf16[1024,64]{1,0:T(8,128)(2,1)S(1)}) custom-call(s32[1]{0:T(128)} %bitcast._.me_ref, bf16[64,128]{1,0:T(8,128)(2,1)} %hub_ref.1, s32[8,64]{1,0:T(8,128)} %bitcast.19, s32[8,8,64]{2,1,0:T(8,128)} %bitcast.18), custom_call_target="tpu_custom_call" | custom-call | tf_op jit(solution)/shard_map/pack/pallas_call | solution.py:392
  2.7 7.3 %all-to-all-start = ((bf16[32,36,128]{2,1,0:T(8,128)(2,1)}), bf16[32,36,128]{2,1,0:T(8,128)(2,1)S(1)}, u32[]{:S(2)}, u32[]{:S(2)}) async-start(bf16[32,36,128]{2,1,0:T(8,128)(2,1)} %get-tuple-element.33), calls=%async_computation | async-start | bytes 655360 | tf_op jit(solution)/shard_map/all_to_all | solution.py:368
  10.0 0.0 copy-start.2
  10.0 0.0 copy-start.3
  10.0 0.0 copy-start.4
  10.0 9.6 %local.1 = (f32[6,128,1024]{2,1,0:T(8,128)}, bf16[6,128,1024]{2,1,0:T(8,128)(2,1)S(1)}, f32[6,1,1024]{2,1,0:T(1,128)S(1)}, bf16[512,256]{1,0:T(8,128)(2,1)S(1)},...) custom-call(s32[4,48]{1,0:T(4,128)} %bitcast.20, bf16[6144,128]{1,0:T(8,128)(2,1)} %feats_ref.1, ...), custom_call_target="tpu_custom_call" | custom-call | tf_op jit(solution)/shard_map/local/pallas_call | solution.py:407
  19.6 0.0 copy-start
  19.6 0.0 copy-start.5
  19.6 2.4 %all-to-all-done.recv_ref = bf16[32,36,128]{2,1,0:T(8,128)(2,1)S(1)} async-done(((bf16[32,36,128]{2,1,0:T(8,128)(2,1)}), bf16[32,36,128]{2,1,0:T(8,128)(2,1)S(1)}, u32[]{:S(2)}, u32[]{:S(2)}) %all-to-all-start) | async-done | bytes 294944 | tf_op jit(solution)/shard_map/all_to_all | solution.py:368
  22.0 0.0 copy-start.1
  22.0 0.0 copy-done.2
  22.0 0.0 copy-done.3
  22.0 0.0 copy-done.4
  22.0 16.4 %forward.1 = (bf16[6,128,1024]{2,1,0:T(8,128)(2,1)S(1)}, bf16[6,512,1024]{2,1,0:T(8,128)(2,1)S(1)}, f32[6,176,1024]{2,1,0:T(8,128)S(1)}, bf16[6,1024,1024]{2,1,0...) custom-call(bf16[32,36,128]{2,1,0:T(8,128)(2,1)S(1)} %all-to-all-done.recv_ref, ...), custom_call_target="tpu_custom_call" | custom-call | tf_op jit(solution)/shard_map/forward/pallas_call | solution.py:447
  38.4 10.5 %all_to_all.20.sums_ref = f32[32,1,128]{2,1,0:T(1,128)S(1)} all-to-all(f32[32,1,128]{2,1,0:T(1,128)S(1)} %get-tuple-element.40), channel_id=1, replica_groups=mesh['dom'=32] {'dom'}, dimensions={0} | all-to-all | bytes 32768 | tf_op jit(solution)/shard_map/all_to_all | solution.py:368
  48.9 0.0 copy-done
  48.9 0.0 copy-done.5
  48.9 0.0 copy-done.1
  48.9 8.9 %backward.1 = (f32[16,56,128]{2,1,0:T(8,128)S(1)}, bf16[16,56,128]{2,1,0:T(8,128)(2,1)}, f32[1,1]{1,0:T(1,128)}, bf16[6,128,1024]{2,1,0:T(8,128)(2,1)S(1)}) custom-call(s32[1]{0:T(128)} %bitcast._.me_ref, f32[32,1,128]{2,1,0:T(1,128)S(1)} %all_to_all.20.sums_ref, f32[1,64]{1,0:T(1,128)S(1)} %bitcast.16, f32[6,176,1024]{2,1,0:T(8,128)S(1)} %get-tuple-element.41.pmo_ref, ...), custom_call_target="tpu_custom_call" | custom-call | tf_op jit(solution)/shard_map/backward/pallas_call | solution.py:480
  57.8 0.1 collective-permute-start
  57.9 1.7 %collective-permute-done.recv_ref = bf16[16,56,128]{2,1,0:T(8,128)(2,1)S(1)} collective-permute-done((bf16[16,56,128]{2,1,0:T(8,128)(2,1)}, bf16[16,56,128]{2,1,0:T(8,128)(2,1)S(1)}, u32[]{:S(2)}, u32[]{:S(2)}) %collective-permute-start) | collective-permute-done | bytes 229408 | tf_op jit(solution)/shard_map/ppermute | solution.py:502
  59.6 0.7 pair.1
  60.3 3.5 %all-to-all-start.2 = ((bf16[16,56,128]{2,1,0:T(8,128)(2,1)}), bf16[16,56,128]{2,1,0:T(8,128)(2,1)S(1)}, u32[]{:S(2)}, u32[]{:S(2)}) async-start(bf16[16,56,128]{2,1,0:T(8,128)(2,1)} %pair.1), calls=%async_computation.2 | async-start | bytes 458752 | tf_op jit(solution)/shard_map/all_to_all | solution.py:512
  63.8 6.2 %slots.1 = (bf16[32,32,128]{2,1,0:T(8,128)(2,1)S(1)}, bf16[64,1024]{1,0:T(8,128)(2,1)S(1)}) custom-call(bf16[6,128,1024]{2,1,0:T(8,128)(2,1)S(1)} %get-tuple-element.50.dsum_ref, bf16[6,1024,1024]{2,1,0:T(8,128)(2,1)} %get-tuple-element.51.m_ref, bf16[1024,64]{1,0:T(8,128)(2,1)S(1)} %get-tuple-element.52.place_ref), custom_call_target="tpu_custom_call" | custom-call | tf_op jit(solution)/shard_map/slots/pallas_call | solution.py:517
  70.1 3.5 %all-to-all-done.2.recv_ref = bf16[16,56,128]{2,1,0:T(8,128)(2,1)S(1)} async-done(((bf16[16,56,128]{2,1,0:T(8,128)(2,1)}), bf16[16,56,128]{2,1,0:T(8,128)(2,1)S(1)}, u32[]{:S(2)}, u32[]{:S(2)}) %all-to-all-start.2) | async-done | bytes 229408 | tf_op jit(solution)/shard_map/all_to_all | solution.py:512
  73.6 0.1 reduce.1
  73.7 17.8 %all_to_all.21.recv_ref = bf16[32,60,128]{2,1,0:T(8,128)(2,1)S(1)} all-to-all(bf16[32,60,128]{2,1,0:T(8,128)(2,1)S(1)} %reduce.1), channel_id=1, replica_groups=mesh['dom'=32] {'dom'}, dimensions={0} | all-to-all | bytes 983040 | tf_op jit(solution)/shard_map/all_to_all | solution.py:368
  91.5 0.0 collective-permute-start.1
  91.5 1.9 %collective-permute-done.1.other_ref = bf16[32,60,128]{2,1,0:T(8,128)(2,1)S(1)} collective-permute-done((bf16[32,60,128]{2,1,0:T(8,128)(2,1)S(1)}, bf16[32,60,128]{2,1,0:T(8,128)(2,1)S(1)}, u32[]{:S(2)}, u32[]{:S(2)}) %collective-permute-start.1) | collective-permute-done | bytes 491552 | tf_op jit(solution)/shard_map/ppermute | solution.py:536
  93.4 1.1 %final.1 = (f32[128,512]{1,0:T(8,128)}, f32[128,512]{1,0:T(8,128)}, f32[4,128]{1,0:T(4,128)}, f32[172,512]{1,0:T(8,128)}, f32[64,128]{1,0:T(8,128)}) custom-call(s32[1]{0:T(128)} %bitcast._.me_ref, bf16[32,60,128]{2,1,0:T(8,128)(2,1)S(1)} %all_to_all.21.recv_ref, bf16[32,60,128]{2,1,0:T(8,128)(2,1)S(1)} %collective-permute-done.1.other_ref, ...), custom_call_target="tpu_custom_call" | custom-call | tf_op jit(solution)/shard_map/final/pallas_call | solution.py:537
Async XLA Ops:
  2.7 19.3 %all-to-all-start = ((bf16[32,36,128]{2,1,0:T(8,128)(2,1)}), bf16[32,36,128]{2,1,0:T(8,128)(2,1)S(1)}, u32[]{:S(2)}, u32[]{:S(2)}) async-start(bf16[32,36,128]{2,1,0:T(8,128)(2,1)} %get-tuple-element.33), calls=%async_computation | async-start | bytes 655360 | tf_op jit(solution)/shard_map/all_to_all | solution.py:368
  10.0 12.0 %copy-start.2 = (s32[6144]{0:T(1024)S(1)}, s32[6144]{0:T(1024)}, u32[]{:S(2)}) copy-start(s32[6144]{0:T(1024)} %param.20) | copy-start | bytes 73732
  10.0 12.0 %copy-start.3 = (s32[6144]{0:T(1024)S(1)}, s32[6144]{0:T(1024)}, u32[]{:S(2)}) copy-start(s32[6144]{0:T(1024)} %param.21) | copy-start | bytes 73732
  10.0 12.0 %copy-start.4 = (s32[6144]{0:T(1024)S(1)}, s32[6144]{0:T(1024)}, u32[]{:S(2)}) copy-start(s32[6144]{0:T(1024)} %param.22) | copy-start | bytes 73732
  19.6 29.3 %copy-start = (bf16[128,512]{1,0:T(8,128)(2,1)S(1)}, bf16[128,512]{1,0:T(8,128)(2,1)}, u32[]{:S(2)}) copy-start(bf16[128,512]{1,0:T(8,128)(2,1)} %wn_ref.3) | copy-start | bytes 393220
  19.6 29.3 %copy-start.5 = (f32[64]{0:T(128)S(1)}, f32[64]{0:T(128)}, u32[]{:S(2)}) copy-start(f32[64]{0:T(128)} %param.27) | copy-start | bytes 772
  22.0 26.9 %copy-start.1 = (bf16[512,176]{1,0:T(8,128)(2,1)S(1)}, bf16[512,176]{1,0:T(8,128)(2,1)}, u32[]{:S(2)}) copy-start(bf16[512,176]{1,0:T(8,128)(2,1)} %get-tuple-element.46.wc_ref) | copy-start | bytes 540676
  57.8 1.8 %collective-permute-start = (bf16[16,56,128]{2,1,0:T(8,128)(2,1)}, bf16[16,56,128]{2,1,0:T(8,128)(2,1)S(1)}, u32[]{:S(2)}, u32[]{:S(2)}) collective-permute-start(bf16[16,56,128]{2,1,0:T(8,128)(2,1)} %get-tuple-element.49), channel_id=1, source_target_pairs={{0,1},{1,0},{2,3},{3,2},{4,5},{5,4},{6,7},{7,6},{8,9},{9,8},{10,11... | collective-permute-start | bytes 688136 | tf_op jit(solution)/shard_map/ppermute | solution.py:502
  60.3 13.3 %all-to-all-start.2 = ((bf16[16,56,128]{2,1,0:T(8,128)(2,1)}), bf16[16,56,128]{2,1,0:T(8,128)(2,1)S(1)}, u32[]{:S(2)}, u32[]{:S(2)}) async-start(bf16[16,56,128]{2,1,0:T(8,128)(2,1)} %pair.1), calls=%async_computation.2 | async-start | bytes 458752 | tf_op jit(solution)/shard_map/all_to_all | solution.py:512
  91.5 1.9 %collective-permute-start.1 = (bf16[32,60,128]{2,1,0:T(8,128)(2,1)S(1)}, bf16[32,60,128]{2,1,0:T(8,128)(2,1)S(1)}, u32[]{:S(2)}, u32[]{:S(2)}) collective-permute-start(bf16[32,60,128]{2,1,0:T(8,128)(2,1)S(1)} %all_to_all.21.recv_ref), channel_id=1, source_target_pairs={{0,1},{1,0},{2,3},{3,2},{4,5},{5,4},{6,7},{7,6},{8,9},{9,8},{10,11... | collective-permute-start | bytes 1474568 | tf_op jit(solution)/shard_map/ppermute | solution.py:536

commit v6 on v5

--- a/solution.py
+++ b/solution.py
@@ -182,7 +182,7 @@
             value_of[:, at] = jnp.left_shift(1, ((target >> 4) & 7) * 4)
         src[width:, :] = jnp.ones((16, slots), BF16)
 
-    chunk = 256
+    chunk = 512
     for c in range(slots // chunk):
         at = slice(c * chunk, (c + 1) * chunk)
         word = [jnp.broadcast_to(word_of[k : k + 1, at], (16, chunk)) for k in range(links)]

time: 95.1 us -> 95.1 us (level)
  no operation moved by 1% of the time
where the time goes in v6:
time: 95.1 us; the launch traced here: 94.5 us
  Pallas kernels  45.1 us (47%)
  blocking collectives  28.3 us (30%)
  starting transfers between devices  10.9 us (11%)
  waiting for transfers between devices  9.5 us (10%)
    all_to_all x2, blocking collectives, exchange(): return lax.all_to_all(x, 'dom', split_axis=0, concat_axis=0, tiled=True)  28.3 us
    pallas_call x1, Pallas kernels, on_device(): pl.pallas_call(functools.partial(forward_kernel, n, cap, links, classes,...  16.4 us
    pallas_call x1, Pallas kernels, on_device(): pl.pallas_call(functools.partial(local_kernel, tiles), name='local', grid...  9.59 us
    pallas_call x1, Pallas kernels, on_device(): pl.pallas_call(functools.partial(backward_kernel, span), name='backward',...  8.87 us
    all_to_all x1, starting transfers between devices, exchange(): return lax.all_to_all(x, 'dom', split_axis=0, concat_axis=0, tiled=True)  7.3 us
    pallas_call x1, Pallas kernels, on_device(): pl.pallas_call(slot_kernel, name='slots', grid=(steps // blocks,), in_spe...  6.23 us
    all_to_all x1, waiting for transfers between devices, on_device(): lax.all_to_all(paired, 'dom', split_axis=0, concat_axis=0, tiled=True, ax...  3.55 us
    all_to_all x1, starting transfers between devices, on_device(): lax.all_to_all(paired, 'dom', split_axis=0, concat_axis=0, tiled=True, ax...  3.53 us
  transfers between devices with their start and end apart: 4, of which 4 were waited for; matrix products, arithmetic and copies ran while one was open for 0% of the time, Pallas kernels for 17%

profile of v6, /device:TPU:0, one launch (start us, length us, event | category | flops | bytes accessed | tf_op | source)
XLA Modules:
  0.0 94.5 jit_solution(9612166194263683152)
XLA Ops:
  0.6 2.1 %pack.1 = (bf16[32,36,128]{2,1,0:T(8,128)(2,1)}, bf16[1024,64]{1,0:T(8,128)(2,1)S(1)}) custom-call(s32[1]{0:T(128)} %bitcast._.me_ref, bf16[64,128]{1,0:T(8,128)(2,1)} %hub_ref.1, s32[8,64]{1,0:T(8,128)} %bitcast.19, s32[8,8,64]{2,1,0:T(8,128)} %bitcast.18), custom_call_target="tpu_custom_call" | custom-call | tf_op jit(solution)/shard_map/pack/pallas_call | solution.py:392
  2.7 7.3 %all-to-all-start = ((bf16[32,36,128]{2,1,0:T(8,128)(2,1)}), bf16[32,36,128]{2,1,0:T(8,128)(2,1)S(1)}, u32[]{:S(2)}, u32[]{:S(2)}) async-start(bf16[32,36,128]{2,1,0:T(8,128)(2,1)} %get-tuple-element.33), calls=%async_computation | async-start | bytes 655360 | tf_op jit(solution)/shard_map/all_to_all | solution.py:368
  10.0 0.0 copy-start.2
  10.0 0.0 copy-start.3
  10.0 0.0 copy-start.4
  10.0 9.6 %local.1 = (f32[6,128,1024]{2,1,0:T(8,128)}, bf16[6,128,1024]{2,1,0:T(8,128)(2,1)S(1)}, f32[6,1,1024]{2,1,0:T(1,128)S(1)}, bf16[512,256]{1,0:T(8,128)(2,1)S(1)},...) custom-call(s32[4,48]{1,0:T(4,128)} %bitcast.20, bf16[6144,128]{1,0:T(8,128)(2,1)} %feats_ref.1, ...), custom_call_target="tpu_custom_call" | custom-call | tf_op jit(solution)/shard_map/local/pallas_call | solution.py:407
  19.6 0.0 copy-start
  19.6 0.0 copy-start.5
  19.6 2.4 %all-to-all-done.recv_ref = bf16[32,36,128]{2,1,0:T(8,128)(2,1)S(1)} async-done(((bf16[32,36,128]{2,1,0:T(8,128)(2,1)}), bf16[32,36,128]{2,1,0:T(8,128)(2,1)S(1)}, u32[]{:S(2)}, u32[]{:S(2)}) %all-to-all-start) | async-done | bytes 294944 | tf_op jit(solution)/shard_map/all_to_all | solution.py:368
  22.0 0.0 copy-start.1
  22.0 0.0 copy-done.2
  22.0 0.0 copy-done.3
  22.0 0.0 copy-done.4
  22.0 16.4 %forward.1 = (bf16[6,128,1024]{2,1,0:T(8,128)(2,1)S(1)}, bf16[6,512,1024]{2,1,0:T(8,128)(2,1)S(1)}, f32[6,176,1024]{2,1,0:T(8,128)S(1)}, bf16[6,1024,1024]{2,1,0...) custom-call(bf16[32,36,128]{2,1,0:T(8,128)(2,1)S(1)} %all-to-all-done.recv_ref, ...), custom_call_target="tpu_custom_call" | custom-call | tf_op jit(solution)/shard_map/forward/pallas_call | solution.py:447
  38.4 10.5 %all_to_all.20.sums_ref = f32[32,1,128]{2,1,0:T(1,128)S(1)} all-to-all(f32[32,1,128]{2,1,0:T(1,128)S(1)} %get-tuple-element.40), channel_id=1, replica_groups=mesh['dom'=32] {'dom'}, dimensions={0} | all-to-all | bytes 32768 | tf_op jit(solution)/shard_map/all_to_all | solution.py:368
  48.9 0.0 copy-done
  48.9 0.0 copy-done.5
  48.9 0.0 copy-done.1
  48.9 8.9 %backward.1 = (f32[16,56,128]{2,1,0:T(8,128)S(1)}, bf16[16,56,128]{2,1,0:T(8,128)(2,1)}, f32[1,1]{1,0:T(1,128)}, bf16[6,128,1024]{2,1,0:T(8,128)(2,1)S(1)}) custom-call(s32[1]{0:T(128)} %bitcast._.me_ref, f32[32,1,128]{2,1,0:T(1,128)S(1)} %all_to_all.20.sums_ref, f32[1,64]{1,0:T(1,128)S(1)} %bitcast.16, f32[6,176,1024]{2,1,0:T(8,128)S(1)} %get-tuple-element.41.pmo_ref, ...), custom_call_target="tpu_custom_call" | custom-call | tf_op jit(solution)/shard_map/backward/pallas_call | solution.py:480
  57.8 0.1 collective-permute-start
  57.9 1.7 %collective-permute-done.recv_ref = bf16[16,56,128]{2,1,0:T(8,128)(2,1)S(1)} collective-permute-done((bf16[16,56,128]{2,1,0:T(8,128)(2,1)}, bf16[16,56,128]{2,1,0:T(8,128)(2,1)S(1)}, u32[]{:S(2)}, u32[]{:S(2)}) %collective-permute-start) | collective-permute-done | bytes 229408 | tf_op jit(solution)/shard_map/ppermute | solution.py:502
  59.6 0.7 pair.1
  60.3 3.5 %all-to-all-start.2 = ((bf16[16,56,128]{2,1,0:T(8,128)(2,1)}), bf16[16,56,128]{2,1,0:T(8,128)(2,1)S(1)}, u32[]{:S(2)}, u32[]{:S(2)}) async-start(bf16[16,56,128]{2,1,0:T(8,128)(2,1)} %pair.1), calls=%async_computation.2 | async-start | bytes 458752 | tf_op jit(solution)/shard_map/all_to_all | solution.py:512
  63.8 6.2 %slots.1 = (bf16[32,32,128]{2,1,0:T(8,128)(2,1)S(1)}, bf16[64,1024]{1,0:T(8,128)(2,1)S(1)}) custom-call(bf16[6,128,1024]{2,1,0:T(8,128)(2,1)S(1)} %get-tuple-element.50.dsum_ref, bf16[6,1024,1024]{2,1,0:T(8,128)(2,1)} %get-tuple-element.51.m_ref, bf16[1024,64]{1,0:T(8,128)(2,1)S(1)} %get-tuple-element.52.place_ref), custom_call_target="tpu_custom_call" | custom-call | tf_op jit(solution)/shard_map/slots/pallas_call | solution.py:517
  70.1 3.5 %all-to-all-done.2.recv_ref = bf16[16,56,128]{2,1,0:T(8,128)(2,1)S(1)} async-done(((bf16[16,56,128]{2,1,0:T(8,128)(2,1)}), bf16[16,56,128]{2,1,0:T(8,128)(2,1)S(1)}, u32[]{:S(2)}, u32[]{:S(2)}) %all-to-all-start.2) | async-done | bytes 229408 | tf_op jit(solution)/shard_map/all_to_all | solution.py:512
  73.6 0.1 reduce.1
  73.7 17.8 %all_to_all.21.recv_ref = bf16[32,60,128]{2,1,0:T(8,128)(2,1)S(1)} all-to-all(bf16[32,60,128]{2,1,0:T(8,128)(2,1)S(1)} %reduce.1), channel_id=1, replica_groups=mesh['dom'=32] {'dom'}, dimensions={0} | all-to-all | bytes 983040 | tf_op jit(solution)/shard_map/all_to_all | solution.py:368
  91.5 0.0 collective-permute-start.1
  91.5 1.9 %collective-permute-done.1.other_ref = bf16[32,60,128]{2,1,0:T(8,128)(2,1)S(1)} collective-permute-done((bf16[32,60,128]{2,1,0:T(8,128)(2,1)S(1)}, bf16[32,60,128]{2,1,0:T(8,128)(2,1)S(1)}, u32[]{:S(2)}, u32[]{:S(2)}) %collective-permute-start.1) | collective-permute-done | bytes 491552 | tf_op jit(solution)/shard_map/ppermute | solution.py:536
  93.4 1.1 %final.1 = (f32[128,512]{1,0:T(8,128)}, f32[128,512]{1,0:T(8,128)}, f32[4,128]{1,0:T(4,128)}, f32[172,512]{1,0:T(8,128)}, f32[64,128]{1,0:T(8,128)}) custom-call(s32[1]{0:T(128)} %bitcast._.me_ref, bf16[32,60,128]{2,1,0:T(8,128)(2,1)S(1)} %all_to_all.21.recv_ref, bf16[32,60,128]{2,1,0:T(8,128)(2,1)S(1)} %collective-permute-done.1.other_ref, ...), custom_call_target="tpu_custom_call" | custom-call | tf_op jit(solution)/shard_map/final/pallas_call | solution.py:537
Async XLA Ops:
  2.7 19.3 %all-to-all-start = ((bf16[32,36,128]{2,1,0:T(8,128)(2,1)}), bf16[32,36,128]{2,1,0:T(8,128)(2,1)S(1)}, u32[]{:S(2)}, u32[]{:S(2)}) async-start(bf16[32,36,128]{2,1,0:T(8,128)(2,1)} %get-tuple-element.33), calls=%async_computation | async-start | bytes 655360 | tf_op jit(solution)/shard_map/all_to_all | solution.py:368
  10.0 12.0 %copy-start.2 = (s32[6144]{0:T(1024)S(1)}, s32[6144]{0:T(1024)}, u32[]{:S(2)}) copy-start(s32[6144]{0:T(1024)} %param.20) | copy-start | bytes 73732
  10.0 12.0 %copy-start.3 = (s32[6144]{0:T(1024)S(1)}, s32[6144]{0:T(1024)}, u32[]{:S(2)}) copy-start(s32[6144]{0:T(1024)} %param.21) | copy-start | bytes 73732
  10.0 12.0 %copy-start.4 = (s32[6144]{0:T(1024)S(1)}, s32[6144]{0:T(1024)}, u32[]{:S(2)}) copy-start(s32[6144]{0:T(1024)} %param.22) | copy-start | bytes 73732
  19.6 29.3 %copy-start = (bf16[128,512]{1,0:T(8,128)(2,1)S(1)}, bf16[128,512]{1,0:T(8,128)(2,1)}, u32[]{:S(2)}) copy-start(bf16[128,512]{1,0:T(8,128)(2,1)} %wn_ref.3) | copy-start | bytes 393220
  19.6 29.3 %copy-start.5 = (f32[64]{0:T(128)S(1)}, f32[64]{0:T(128)}, u32[]{:S(2)}) copy-start(f32[64]{0:T(128)} %param.27) | copy-start | bytes 772
  22.0 26.9 %copy-start.1 = (bf16[512,176]{1,0:T(8,128)(2,1)S(1)}, bf16[512,176]{1,0:T(8,128)(2,1)}, u32[]{:S(2)}) copy-start(bf16[512,176]{1,0:T(8,128)(2,1)} %get-tuple-element.46.wc_ref) | copy-start | bytes 540676
  57.8 1.8 %collective-permute-start = (bf16[16,56,128]{2,1,0:T(8,128)(2,1)}, bf16[16,56,128]{2,1,0:T(8,128)(2,1)S(1)}, u32[]{:S(2)}, u32[]{:S(2)}) collective-permute-start(bf16[16,56,128]{2,1,0:T(8,128)(2,1)} %get-tuple-element.49), channel_id=1, source_target_pairs={{0,1},{1,0},{2,3},{3,2},{4,5},{5,4},{6,7},{7,6},{8,9},{9,8},{10,11... | collective-permute-start | bytes 688136 | tf_op jit(solution)/shard_map/ppermute | solution.py:502
  60.3 13.3 %all-to-all-start.2 = ((bf16[16,56,128]{2,1,0:T(8,128)(2,1)}), bf16[16,56,128]{2,1,0:T(8,128)(2,1)S(1)}, u32[]{:S(2)}, u32[]{:S(2)}) async-start(bf16[16,56,128]{2,1,0:T(8,128)(2,1)} %pair.1), calls=%async_computation.2 | async-start | bytes 458752 | tf_op jit(solution)/shard_map/all_to_all | solution.py:512
  91.5 1.9 %collective-permute-start.1 = (bf16[32,60,128]{2,1,0:T(8,128)(2,1)S(1)}, bf16[32,60,128]{2,1,0:T(8,128)(2,1)S(1)}, u32[]{:S(2)}, u32[]{:S(2)}) collective-permute-start(bf16[32,60,128]{2,1,0:T(8,128)(2,1)S(1)} %all_to_all.21.recv_ref), channel_id=1, source_target_pairs={{0,1},{1,0},{2,3},{3,2},{4,5},{5,4},{6,7},{7,6},{8,9},{9,8},{10,11... | collective-permute-start | bytes 1474568 | tf_op jit(solution)/shard_map/ppermute | solution.py:536
